TPU v7x, 512 devices: a whole 4x4x16 slice. The times are simulated.
512 devices in a mesh: grp: 16 (over x, y), dev: 32 (over z, core).
Axes of the slice: x: 4, y: 4, z: 16, core: 2. Of those that a mesh axis runs over, the one named last changes fastest.
Arguments:
- coords: float32 [3, 65536], P(None, ('grp', 'dev')), may hold values from 0 to 1
- field: float32 [65536, 256], P(('grp', 'dev')), may hold values from -6 to 6
- observed: float32 [65536, 256], P(('grp', 'dev')), may hold values from -9 to 9
- pair_owner: int32 [16, 32], replicated, may hold values from 0 to 31, as said below
- cond_list: int32 [1024, 8], replicated, may hold values from 0 to 1023, as said below
- cond_mask: int32 [1024, 8], replicated, may hold values from 0 to 1, as said below
Outputs:
- field_out: float32 [65536, 256], P(('grp', 'dev'))
- last_grad: float32 [65536, 256], P(('grp', 'dev'))
Inputs may be any that keep to these rules, and one draw needn't show every extreme that they name: `pair_owner`: each row is a permutation of the device indices. `cond_list`: a used slot s < 6 of block b names an earlier block of b's group, a used slot s >= 6 a block of the group before; padded slots hold 0; for every group g and devices p, q of it, the used slots of the blocks stored on device p of group g and of those stored on device p of group g + 1 that name blocks stored on device q of group g name one block at most, and no more than one slot names it; this bound is reached. `cond_mask`: blocks of the first group and early blocks of a group have padded slots.
All inputs are finite; a program needn't handle non-finite values.
Results may differ from a plain program's by a relative error of at most 0.0017.
Values may be sent and summed in bfloat16 or wider, within the bound.
A program may use at most 64 MiB of HBM per device.

v0:
```python
import jax
import jax.numpy as jnp
from jax import lax
from jax.sharding import PartitionSpec as P

NCOND = 8
NSAME = 6
STEPS = 2


HIGH = lax.Precision.HIGHEST
LENGTH_SCALE = 0.35
NUGGET = 0.5
STEP_SIZE = 0.3


def shifted(block, axis, distance):
    devices = range(lax.axis_size(axis))
    route = [(i - distance, i) for i in devices if i - distance in devices]
    return lax.ppermute(block, axis, route)


def kernel_of(first, second):
    dist_sq = jnp.zeros((first.shape[1], second.shape[1]), jnp.float32)
    for coord in range(3):
        diff = first[coord][:, None] - second[coord][None, :]
        dist_sq = dist_sq + diff * diff
    return jnp.exp(-jnp.sqrt(dist_sq) / LENGTH_SCALE)


def factor_block(own_x, cond_x, point_mask):
    kcc = kernel_of(cond_x, cond_x) * point_mask[:, None] * point_mask[None, :]
    kcc = kcc + jnp.diag(NUGGET * point_mask + (1.0 - point_mask))
    kci = kernel_of(cond_x, own_x) * point_mask[:, None]
    count = own_x.shape[1]
    kii = kernel_of(own_x, own_x) + NUGGET * jnp.eye(count, dtype=jnp.float32)
    lower = jnp.linalg.cholesky(kcc)
    whiten = lax.linalg.triangular_solve(lower, kci, left_side=True, lower=True)
    regress = lax.linalg.triangular_solve(
        lower, whiten, left_side=True, lower=True, transpose_a=True
    )
    cond_cov = kii - jnp.dot(whiten.T, whiten, precision=HIGH)
    low_cov = jnp.linalg.cholesky(cond_cov)
    inv_low = lax.linalg.triangular_solve(
        low_cov, jnp.eye(count, dtype=jnp.float32), left_side=True, lower=True
    )
    precision = jnp.dot(inv_low.T, inv_low, precision=HIGH)
    return (regress, precision)


def body(coords, field, observed, pair_owner, cond_list, cond_mask):
    groups = lax.axis_size("grp")
    group_members = lax.axis_size("dev")
    my_group = lax.axis_index("grp")
    my_member = lax.axis_index("dev")
    points = field.shape[0] // 2
    out_cols = field.shape[1]
    cross_covariance = NCOND - NSAME
    member_ids = jnp.arange(group_members, dtype=jnp.int32)
    halves = jnp.arange(2, dtype=jnp.int32)
    inverse_factor = jnp.sum(
        jnp.where(
            pair_owner[:, :, None] == member_ids[None, None, :], member_ids[None, :, None], 0
        ),
        axis=1,
    )
    all_lists = cond_list.reshape(groups, group_members, 2, NCOND)
    all_masks = cond_mask.reshape(groups, group_members, 2, NCOND)
    next_group = jnp.minimum(my_group + 1, groups - 1)
    has_next = (my_group + 1 < groups).astype(jnp.int32)
    owner_here = pair_owner[my_group]
    base_id = my_group * 2 * group_members

    def locate(targets):
        pair_idx = jnp.clip((targets - base_id) // 2, 0, group_members - 1)
        return (owner_here[pair_idx], targets % 2)

    here_lists = all_lists[my_group][inverse_factor[my_group]]
    here_masks = all_masks[my_group][inverse_factor[my_group]]
    next_lists = all_lists[next_group][inverse_factor[next_group]][:, :, NSAME:]
    next_masks = all_masks[next_group][inverse_factor[next_group]][:, :, NSAME:] * has_next
    same_owner, same_half = locate(here_lists[:, :, :NSAME])
    fwd_owner, fwd_half = locate(next_lists)
    same_hit = (here_masks[:, :, :NSAME] * (same_owner == my_member))[..., None] * (
        same_half[..., None] == halves
    )
    fwd_hit = (next_masks * (fwd_owner == my_member))[..., None] * (fwd_half[..., None] == halves)
    selector = (jnp.sum(same_hit, axis=(1, 2)) + jnp.sum(fwd_hit, axis=(1, 2))).astype(jnp.float32)
    select_bf = selector.astype(jnp.bfloat16)
    same_valid = here_masks[my_member][:, :NSAME].reshape(-1).astype(jnp.float32)
    fwd_valid = next_masks[my_member].reshape(-1).astype(jnp.float32)
    req_owner = jnp.concatenate(
        [same_owner[my_member].reshape(-1), fwd_owner[my_member].reshape(-1)]
    )
    req_half = jnp.concatenate([same_half[my_member].reshape(-1), fwd_half[my_member].reshape(-1)])
    req_valid = jnp.concatenate([same_valid, fwd_valid])
    req_row = 2 * req_owner + req_half
    my_mask = here_masks[my_member].astype(jnp.float32)
    onehot_same = (
        (same_owner[my_member].reshape(-1)[:, None] == member_ids[None, :]) * same_valid[:, None]
    ).astype(jnp.bfloat16)
    onehot_fwd = (
        (fwd_owner[my_member].reshape(-1)[:, None] == member_ids[None, :]) * fwd_valid[:, None]
    ).astype(jnp.bfloat16)
    own_x = coords.reshape(3, 2, points).transpose(1, 0, 2)
    send_x = (
        selector[:, 0, None, None] * own_x[0][None] + selector[:, 1, None, None] * own_x[1][None]
    )
    recv_x = lax.all_to_all(send_x, "dev", split_axis=0, concat_axis=0, tiled=True)
    got_x = recv_x[req_owner]
    same_x = got_x[: 2 * NSAME].reshape(2, NSAME, 3, points)
    lift_x = shifted(got_x[2 * NSAME :].reshape(2, cross_covariance, 3, points), "grp", 1)
    cond_x = (
        jnp.concatenate([same_x, lift_x], axis=1)
        .transpose(0, 2, 1, 3)
        .reshape(2, 3, NCOND * points)
    )
    point_mask = jnp.repeat(my_mask, points, axis=1)
    regress, precision = jax.vmap(factor_block)(own_x, cond_x, point_mask)
    state = field.reshape(2, points, out_cols)
    target = observed.reshape(2, points, out_cols)
    slot_mask = my_mask[:, :, None, None]
    grad = jnp.zeros_like(state)
    for step_idx in range(STEPS):
        rounded = state.astype(jnp.bfloat16)
        piece = lax.all_gather(rounded, "dev", axis=0, tiled=True)
        rows = jnp.arange(piece.shape[0], dtype=jnp.int32)
        hit = ((req_row[:, None] == rows[None, :]) * req_valid[:, None]).astype(jnp.bfloat16)
        got = jnp.einsum("rn,npo->rpo", hit, piece, preferred_element_type=jnp.float32).astype(
            jnp.bfloat16
        )
        same = got[: 2 * NSAME].reshape(2, NSAME, points, out_cols)
        lifted = shifted(got[2 * NSAME :].reshape(2, cross_covariance, points, out_cols), "grp", 1)
        cond = jnp.concatenate([same, lifted], axis=1).astype(jnp.float32) * slot_mask
        cond = cond.reshape(2, NCOND * points, out_cols)
        resid = state - jnp.einsum("hnp,hno->hpo", regress, cond, precision=HIGH)
        scaled = jnp.einsum("hpq,hqo->hpo", precision, resid, precision=HIGH)
        back = jnp.einsum("hnp,hpo->hno", regress, scaled, precision=HIGH).reshape(
            2, NCOND, points, out_cols
        )
        back = (back * slot_mask).astype(jnp.bfloat16)
        dropped = shifted(back[:, NSAME:], "grp", -1)
        outgo = jnp.einsum(
            "rq,rpo->qpo",
            onehot_same,
            back[:, :NSAME].reshape(2 * NSAME, points, out_cols),
            preferred_element_type=jnp.float32,
        )
        outgo = outgo + jnp.einsum(
            "rq,rpo->qpo",
            onehot_fwd,
            dropped.reshape(2 * cross_covariance, points, out_cols),
            preferred_element_type=jnp.float32,
        )
        returned = lax.all_to_all(
            outgo.astype(jnp.bfloat16), "dev", split_axis=0, concat_axis=0, tiled=True
        )
        incoming = jnp.einsum(
            "qh,qpo->hpo", select_bf, returned, preferred_element_type=jnp.float32
        )
        grad = jnp.tanh(target - state) - (scaled - incoming)
        state = state + STEP_SIZE * grad
    return (state.reshape(2 * points, out_cols), grad.reshape(2 * points, out_cols))


def solution(mesh):
    placed = (
        P(None, ("grp", "dev")),
        P(("grp", "dev"), None),
        P(("grp", "dev"), None),
        P(),
        P(),
        P(),
    )
    return jax.shard_map(
        body,
        mesh=mesh,
        in_specs=placed,
        out_specs=(P(("grp", "dev"), None), P(("grp", "dev"), None)),
        check_vma=False,
    )
```

profile of v0, /device:TPU:3, one launch (start us, length us, event | category | flops | bytes accessed | tf_op | source)
XLA Modules:
  0.0 595.5 jit_solution(17836235499688568392)
XLA Ops:
  7.2 0.8 select_reduce_fusion
  8.0 1.0 copy.136
  9.0 1.0 copy.134
  9.9 0.7 fusion.113
  11.6 2.7 gather_fusion.1
  15.5 1.2 gather_fusion.4
  19.0 0.7 reshape.479
  19.7 15.9 %all-to-all-start = ((f32[32,1,192]{2,1,0:T(1,128)}), f32[32,1,192]{2,1,0:T(1,128)S(1)}, u32[]{:S(2)}, u32[]{:S(2)}) async-start(f32[32,1,192]{2,1,0:T(1,128)} %reshape.479), calls=%async_computation | async-start | bytes 65536 | tf_op jit(solution)/shard_map/all_to_all | solution.py:109
  35.7 0.6 convert_element_type.105
  39.4 0.7 pad_maximum_fusion.3
  40.1 7.6 %all-to-all-done = f32[32,1,192]{2,1,0:T(1,128)S(1)} async-done(((f32[32,1,192]{2,1,0:T(1,128)}), f32[32,1,192]{2,1,0:T(1,128)S(1)}, u32[]{:S(2)}, u32[]{:S(2)}) %all-to-all-start) | async-done | bytes 24608 | tf_op jit(solution)/shard_map/all_to_all | solution.py:109
  48.2 0.7 reduce.30
  49.6 3.2 collective-permute-start
  52.8 0.7 fusion.115
  53.5 2.6 collective-permute-done
  56.8 3.4 add_multiply_fusion
  60.3 1.3 copy-done
  61.6 24.0 %custom-call.43 = f32[2,128,128]{2,1,0:T(8,128)S(1)} custom-call(f32[2,128,128]{2,1,0:T(8,128)S(1)} %cholesky.314), custom_call_target="Cholesky" | custom-call | tf_op jit(solution)/shard_map/vmap(jit(cholesky))/cholesky | solution.py:37
  85.8 19.7 %custom-call.44 = f32[2,1,128,128]{2,3,1,0:T(8,128)S(1)} custom-call(f32[2,1,128,128]{3,2,1,0:T(8,128)S(1)} %select_bitcast_fusion.2), custom_call_target="InvertDiagBlocksLowerTriangular" | custom-call | tf_op jit(solution)/shard_map/vmap(jit(cholesky))/cholesky | solution.py:37
  105.5 1.5 constant_dynamic-update-slice_fusion.3
  107.0 1.5 convolution_subtract_fusion
  108.6 23.5 %custom-call.45 = f32[2,128,128]{2,1,0:T(8,128)S(1)} custom-call(f32[2,128,128]{2,1,0:T(8,128)S(1)} %cholesky.318), custom_call_target="Cholesky" | custom-call | tf_op jit(solution)/shard_map/vmap(jit(cholesky))/cholesky | solution.py:37
  132.1 19.8 %custom-call.46 = f32[2,1,128,128]{2,3,1,0:T(8,128)S(1)} custom-call(f32[2,1,128,128]{3,2,1,0:T(8,128)S(1)} %get-tuple-element.39), custom_call_target="InvertDiagBlocksLowerTriangular" | custom-call | tf_op jit(solution)/shard_map/vmap(jit(cholesky))/cholesky | solution.py:37
  152.3 1.6 convolution_subtract_fusion.1
  153.9 23.5 %custom-call.47 = f32[2,128,128]{2,1,0:T(8,128)S(1)} custom-call(f32[2,128,128]{2,1,0:T(8,128)S(1)} %cholesky.323), custom_call_target="Cholesky" | custom-call | tf_op jit(solution)/shard_map/vmap(jit(cholesky))/cholesky | solution.py:37
  177.4 19.7 %custom-call.48 = f32[2,1,128,128]{2,3,1,0:T(8,128)S(1)} custom-call(f32[2,1,128,128]{3,2,1,0:T(8,128)S(1)} %get-tuple-element.37), custom_call_target="InvertDiagBlocksLowerTriangular" | custom-call | tf_op jit(solution)/shard_map/vmap(jit(cholesky))/cholesky | solution.py:37
  197.3 1.5 convolution_subtract_fusion.2
  198.9 23.7 %custom-call.49 = f32[2,128,128]{2,1,0:T(8,128)S(1)} custom-call(f32[2,128,128]{2,1,0:T(8,128)S(1)} %convolution_subtract_fusion.2), custom_call_target="Cholesky" | custom-call | tf_op jit(solution)/shard_map/vmap(jit(cholesky))/cholesky | solution.py:37
  223.1 1.7 select_select_fusion
  224.8 14.2 %while.1 = (s32[]{:T(128)}, f32[2,512,512]{2,1,0:T(8,128)}, s32[4,2]{0,1:T(2,128)S(1)}, f32[4,2,128,128]{3,2,0,1:T(8,128)}, s32[]{:T(128)}) while((s32[]{:T(128)}, f32[2,512,512]{2,1,0:T(8,128)}, s32[4,2]{0,1:T(2,128)S(1)}, f32[4,2,128,128]{3,2,0,1:T(8,128)}, s32[]{:T(128)}) %tuple.51), condition=%wide.while_cond, body=%wide.while_body.sunk | while | flops 2 | bytes 263777 | solution.py:38
  225.5 2.9 bitcast_dynamic-update-slice_fusion.2
  229.0 2.9 bitcast_dynamic-update-slice_fusion.2
  232.6 2.9 bitcast_dynamic-update-slice_fusion.2
  236.2 2.9 bitcast_dynamic-update-slice_fusion.2
  239.1 79.4 %custom-call.50 = f32[2,4,128,128]{2,3,1,0:T(8,128)S(1)} custom-call(f32[2,4,128,128]{3,2,1,0:T(8,128)} %bitcast.203), custom_call_target="InvertDiagBlocksLowerTriangular" | custom-call | tf_op jit(solution)/shard_map/vmap()/triangular_solve | solution.py:38
  319.1 1.3 convolution_subtract_fusion.6
  320.6 1.4 convolution_subtract_fusion.8
  322.2 1.6 convolution_subtract_fusion.10
  324.8 11.7 %custom-call.51 = f32[2,64,64]{2,1,0:T(8,128)S(1)} custom-call(f32[2,64,64]{2,1,0:T(8,128)S(1)} %fusion.79), custom_call_target="Cholesky" | custom-call | tf_op jit(solution)/shard_map/vmap(jit(cholesky))/cholesky | solution.py:43
  336.8 10.1 %custom-call.52 = f32[2,1,64,64]{2,3,1,0:T(8,128)S(1)} custom-call(f32[2,1,64,64]{3,2,1,0:T(8,128)S(1)} %select_bitcast_fusion.3), custom_call_target="InvertDiagBlocksLowerTriangular" | custom-call | tf_op jit(solution)/shard_map/vmap()/triangular_solve | solution.py:44
  347.5 1.2 convolution_subtract_fusion.5
  349.0 1.3 convolution_subtract_fusion.7
  350.7 1.4 convolution_subtract_fusion.9
  352.5 2.8 fusion.4
  355.4 1.9 collective-permute-start.1
  357.8 5.5 collective-permute-done.1
  363.3 0.9 convolution_subtract_fusion.4
  364.5 1.0 fusion.134
  365.7 1.9 collective-permute-start.2
  368.2 3.2 collective-permute-done.2
  372.6 63.7 %all_to_all.15 = bf16[32,64,256]{2,1,0:T(8,128)(2,1)S(1)} all-to-all(bf16[32,64,256]{2,1,0:T(8,128)(2,1)S(1)} %copy.165), channel_id=1, replica_groups=mesh['grp'=16,'dev'=32] {'dev'}, dimensions={0} | all-to-all | bytes 2097152 | tf_op jit(solution)/shard_map/all_to_all | solution.py:155
  436.3 0.7 fusion.12
  437.0 0.7 fusion.136
  437.7 62.3 %all-gather.5.cloned.1.call-done = bf16[64,64,256]{2,1,0:T(8,128)(2,1)} async-done(((bf16[2,64,256]{2,1,0:T(8,128)(2,1)}), bf16[64,64,256]{2,1,0:T(8,128)(2,1)}) %all-gather.5.cloned.1.call-update) | async-done | bytes 2097168 | tf_op jit(solution)/shard_map/all_gather | solution.py:126
  500.0 2.8 fusion.7
  502.9 3.1 collective-permute-start.3
  506.1 5.5 collective-permute-done.3
  511.7 0.9 convolution_subtract_fusion.3
  512.9 1.0 fusion.133
  514.1 2.6 collective-permute-start.4
  517.2 2.6 collective-permute-done.4
  521.0 65.8 %all_to_all.16 = bf16[32,64,256]{2,1,0:T(8,128)(2,1)S(1)} all-to-all(bf16[32,64,256]{2,1,0:T(8,128)(2,1)S(1)} %copy.173), channel_id=1, replica_groups=mesh['grp'=16,'dev'=32] {'dev'}, dimensions={0} | all-to-all | bytes 2097152 | tf_op jit(solution)/shard_map/all_to_all | solution.py:155
  586.7 0.7 fusion.10
  587.4 0.7 multiply_add_fusion
  (193 shorter events, 22.1 us)
Async XLA Ops:
  15.5 3.2 copy-start.26
  15.5 20.1 %copy-start.1 = (f32[128,256]{1,0:T(8,128)S(1)}, f32[128,256]{1,0:T(8,128)}, u32[]{:S(2)}) copy-start(f32[128,256]{1,0:T(8,128)} %param.7) | copy-start | bytes 393220
  18.7 17.7 %copy-start.14 = (f32[32,2]{0,1:T(2,128)}, f32[32,2]{0,1:T(2,128)S(1)}, u32[]{:S(2)}) copy-start(f32[32,2]{0,1:T(2,128)S(1)} %add_convert_fusion.2) | copy-start | bytes 772
  19.7 28.0 %all-to-all-start = ((f32[32,1,192]{2,1,0:T(1,128)}), f32[32,1,192]{2,1,0:T(1,128)S(1)}, u32[]{:S(2)}, u32[]{:S(2)}) async-start(f32[32,1,192]{2,1,0:T(1,128)} %reshape.479), calls=%async_computation | async-start | bytes 65536 | tf_op jit(solution)/shard_map/all_to_all | solution.py:109
  35.6 316.9 %all-gather.3.cloned.1.call-start = ((), (), s32[]{:S(2)}) async-start(), calls=%async_computation.3 | async-start | bytes 2162688 | tf_op jit(solution)/shard_map/all_gather | solution.py:126
  36.3 463.6 %all-gather.5.cloned.1.call-start = ((), (), s32[]{:S(2)}) async-start(), calls=%async_computation.4 | async-start | bytes 2162688 | tf_op jit(solution)/shard_map/all_gather | solution.py:126
  36.5 2.5 copy-start.12
  38.0 18.2 %copy-start.18 = (s32[12]{0:T(128)}, s32[12]{0:T(128)S(1)}, u32[]{:S(2)}) copy-start(s32[12]{0:T(128)S(1)} %concatenate.79) | copy-start | bytes 148
  38.2 18.1 %copy-start.16 = (s32[4]{0:T(128)}, s32[4]{0:T(128)S(1)}, u32[]{:S(2)}) copy-start(s32[4]{0:T(128)S(1)} %concatenate.80) | copy-start | bytes 52
  39.3 10.3 %copy-start.21 = (bf16[4]{0:T(256)(128)(2,1)}, bf16[4]{0:T(256)(128)(2,1)S(1)}, u32[]{:S(2)}) copy-start(bf16[4]{0:T(256)(128)(2,1)S(1)} %convert_element_type.103) | copy-start | bytes 28
  39.4 10.2 %copy-start.23 = (bf16[12]{0:T(256)(128)(2,1)}, bf16[12]{0:T(256)(128)(2,1)S(1)}, u32[]{:S(2)}) copy-start(bf16[12]{0:T(256)(128)(2,1)S(1)} %convert_element_type.101) | copy-start | bytes 76
  49.6 6.5 %collective-permute-start = (f32[2,2,3,64]{3,1,0,2:T(2,128)S(1)}, f32[2,2,3,64]{3,1,0,2:T(2,128)S(1)}, u32[]{:S(2)}, u32[]{:S(2)}) collective-permute-start(f32[2,2,3,64]{3,1,0,2:T(2,128)S(1)} %copy.141), channel_id=1, source_target_pairs={{0,32},{32,64},{64,96},{96,128},{128,160},{160,192},{192,224},{224... | collective-permute-start | bytes 9224 | tf_op jit(solution)/shard_map/ppermute | solution.py:20
  56.2 0.6 copy-start.6
  56.2 0.6 copy-start.8
  56.2 0.6 copy-start.10
  60.2 1.3 copy-start
  223.1 1.8 copy-start.27
  223.1 95.4 %copy-start.4 = (f32[2,64]{1,0:T(2,128)S(1)}, f32[2,64]{1,0:T(2,128)}, u32[]{:S(2)}) copy-start(f32[2,64]{1,0:T(2,128)} %get-tuple-element.51) | copy-start | bytes 1540
  223.1 95.4 %copy-start.5 = (f32[2,64]{1,0:T(2,128)S(1)}, f32[2,64]{1,0:T(2,128)}, u32[]{:S(2)}) copy-start(f32[2,64]{1,0:T(2,128)} %get-tuple-element.52) | copy-start | bytes 1540
  223.1 95.4 %copy-start.7 = (f32[2,512]{1,0:T(2,128)S(1)}, f32[2,512]{1,0:T(2,128)}, u32[]{:S(2)}) copy-start(f32[2,512]{1,0:T(2,128)} %copy-done.6) | copy-start | bytes 12292
  223.1 95.4 %copy-start.9 = (f32[2,512]{1,0:T(2,128)S(1)}, f32[2,512]{1,0:T(2,128)}, u32[]{:S(2)}) copy-start(f32[2,512]{1,0:T(2,128)} %copy-done.8) | copy-start | bytes 12292
  223.1 95.4 %copy-start.11 = (f32[2,512]{1,0:T(2,128)S(1)}, f32[2,512]{1,0:T(2,128)}, u32[]{:S(2)}) copy-start(f32[2,512]{1,0:T(2,128)} %copy-done.10) | copy-start | bytes 12292
  239.1 97.5 %copy-start.3 = (pred[64,64]{1,0:T(8,128)(4,1)S(1)}, pred[64,64]{1,0:T(8,128)(4,1)}, u32[]{:S(2)}) copy-start(pred[64,64]{1,0:T(8,128)(4,1)} %iota_compare_fusion.7) | copy-start | bytes 12292
  323.9 28.6 %copy-start.20 = (s32[16]{0:T(128)S(1)}, s32[16]{0:T(128)}, u32[]{:S(2)}) copy-start(s32[16]{0:T(128)} %fusion.115) | copy-start | bytes 196
  323.9 28.6 %copy-start.25 = (bf16[16]{0:T(256)(128)(2,1)S(1)}, bf16[16]{0:T(256)(128)(2,1)}, u32[]{:S(2)}) copy-start(bf16[16]{0:T(256)(128)(2,1)} %pad_maximum_fusion.3) | copy-start | bytes 100
  355.4 7.8 %collective-permute-start.1 = (bf16[2,2,64,256]{3,2,1,0:T(8,128)(2,1)S(1)}, bf16[2,2,64,256]{3,2,1,0:T(8,128)(2,1)S(1)}, u32[]{:S(2)}, u32[]{:S(2)}) collective-permute-start(bf16[2,2,64,256]{3,2,1,0:T(8,128)(2,1)S(1)} %bitcast.195), channel_id=1, source_target_pairs={{0,32},{32,64},{64,96},{96,128},{128,160},{160,192},{192,224},{224... | collective-permute-start | bytes 393224 | tf_op jit(solution)/shard_map/ppermute | solution.py:20
  357.8 7.7 %copy-start.13 = (f32[2,8]{1,0:T(2,128)S(1)}, f32[2,8]{1,0:T(2,128)}, u32[]{:S(2)}) copy-start(f32[2,8]{1,0:T(2,128)} %copy-done.12) | copy-start | bytes 196
  364.5 3.2 copy-start.19
  364.5 3.2 copy-start.24
  365.7 5.8 copy-start.17
  365.7 5.8 copy-start.22
  365.7 5.7 collective-permute-start.2
  372.0 64.3 %copy-start.15 = (f32[32,2]{0,1:T(2,128)S(1)}, f32[32,2]{0,1:T(2,128)}, u32[]{:S(2)}) copy-start(f32[32,2]{0,1:T(2,128)} %copy-done.14) | copy-start | bytes 772
  372.6 64.3 %copy-start.2 = (f32[128,256]{1,0:T(8,128)S(1)}, f32[128,256]{1,0:T(8,128)}, u32[]{:S(2)}) copy-start(f32[128,256]{1,0:T(8,128)} %param.8) | copy-start | bytes 393220
  502.9 8.8 %collective-permute-start.3 = (bf16[2,2,64,256]{3,2,1,0:T(8,128)(2,1)S(1)}, bf16[2,2,64,256]{3,2,1,0:T(8,128)(2,1)S(1)}, u32[]{:S(2)}, u32[]{:S(2)}) collective-permute-start(bf16[2,2,64,256]{3,2,1,0:T(8,128)(2,1)S(1)} %bitcast.196), channel_id=1, source_target_pairs={{0,32},{32,64},{64,96},{96,128},{128,160},{160,192},{192,224},{224... | collective-permute-start | bytes 393224 | tf_op jit(solution)/shard_map/ppermute | solution.py:20
  514.1 5.7 collective-permute-start.4
Sparse Core Ops, SparseCore 0:
  39.1 73.2 all-gather.2
  437.8 62.1 all-gather.4
where the time goes:
time: 602 us; the launch traced here: 595 us
  other arithmetic  269 us (45%)
  blocking collectives  129 us (21%)
  waiting for transfers between devices  89.3 us (15%)
  local copies, waits for them, and re-layouts  31.7 us (5%)
  matrix products  31.7 us (5%)
  starting transfers between devices  28.7 us (5%)
  between operations  15.7 us (3%)
    another operation x18, other arithmetic, factor_block(): lower = jnp.linalg.cholesky(kcc)  154 us
    all_to_all x2, blocking collectives, body(): lax.all_to_all(outgo.astype(jnp.bfloat16), 'dev', split_axis=0, concat_ax...  129 us
    another operation x4, other arithmetic, factor_block(): whiten = lax.linalg.triangular_solve(lower, kci, left_side=True, lower=True)  81.8 us
    all_gather x2, waiting for transfers between devices, body(): piece = lax.all_gather(rounded, 'dev', axis=0, tiled=True)  62.3 us
    ppermute x5, waiting for transfers between devices, shifted(): return lax.ppermute(block, axis, route)  19.4 us
    all_to_all x1, starting transfers between devices, body(): lax.all_to_all(send_x, 'dev', split_axis=0, concat_axis=0, tiled=True)  15.9 us
    another operation x12, local copies, waits for them, and re-layouts  14.2 us
    ppermute x5, starting transfers between devices, shifted(): return lax.ppermute(block, axis, route)  12.7 us
  transfers between devices with their start and end apart: 8, of which 7 were waited for; matrix products, arithmetic and copies ran while one was open for 51% of the time, Pallas kernels for 0%

commit v1 on v0

--- a/solution.py
+++ b/solution.py
@@ -1,6 +1,8 @@
 import jax
 import jax.numpy as jnp
 from jax import lax
+from jax.experimental import pallas as pl
+from jax.experimental.pallas import tpu as pltpu
 from jax.sharding import PartitionSpec as P
 
 NCOND = 8
@@ -20,32 +22,98 @@
     return lax.ppermute(block, axis, route)
 
 
-def kernel_of(first, second):
-    dist_sq = jnp.zeros((first.shape[1], second.shape[1]), jnp.float32)
-    for coord in range(3):
-        diff = first[coord][:, None] - second[coord][None, :]
-        dist_sq = dist_sq + diff * diff
-    return jnp.exp(-jnp.sqrt(dist_sq) / LENGTH_SCALE)
-
-
-def factor_block(own_x, cond_x, point_mask):
-    kcc = kernel_of(cond_x, cond_x) * point_mask[:, None] * point_mask[None, :]
-    kcc = kcc + jnp.diag(NUGGET * point_mask + (1.0 - point_mask))
-    kci = kernel_of(cond_x, own_x) * point_mask[:, None]
-    count = own_x.shape[1]
-    kii = kernel_of(own_x, own_x) + NUGGET * jnp.eye(count, dtype=jnp.float32)
-    lower = jnp.linalg.cholesky(kcc)
-    whiten = lax.linalg.triangular_solve(lower, kci, left_side=True, lower=True)
-    regress = lax.linalg.triangular_solve(
-        lower, whiten, left_side=True, lower=True, transpose_a=True
-    )
-    cond_cov = kii - jnp.dot(whiten.T, whiten, precision=HIGH)
-    low_cov = jnp.linalg.cholesky(cond_cov)
-    inv_low = lax.linalg.triangular_solve(
-        low_cov, jnp.eye(count, dtype=jnp.float32), left_side=True, lower=True
-    )
-    precision = jnp.dot(inv_low.T, inv_low, precision=HIGH)
-    return (regress, precision)
+B = 64
+F32 = jnp.float32
+BF = jnp.bfloat16
+
+def dot3(a, b, dims):
+    return lax.dot_general(a, b, (dims, ((), ())), precision=HIGH, preferred_element_type=F32)
+
+
+NN = ((1,), (0,))
+NT = ((1,), (1,))
+
+def diag_pair(block):
+    both = jnp.concatenate([block, block], axis=0)
+    row = lax.broadcasted_iota(jnp.int32, (2 * B, 2 * B), 0)
+    lane = lax.broadcasted_iota(jnp.int32, (2 * B, 2 * B), 1)
+    return jnp.where((row < B) == (lane < B), both, 0.0)
+
+def invert_pair(a):
+    tiles = [a[8 * t : 8 * t + 8] for t in range(8)]
+    lane = lax.broadcasted_iota(jnp.int32, (8, 2 * B), 1)
+    sub = lax.broadcasted_iota(jnp.int32, (8, 2 * B), 0)
+    col = lane % B
+    base = lane - col
+    for k in range(0, B, 2):
+        t, o = k // 8, k % 8
+        c0 = [jnp.take_along_axis(x, base + k, axis=1) for x in tiles]
+        c1 = [jnp.take_along_axis(x, base + k + 1, axis=1) for x in tiles]
+        def bc(x, r):
+            return jnp.broadcast_to(x[r : r + 1], (8, 2 * B))
+        p, q, s = bc(c0[t], o), bc(c0[t], o + 1), bc(c1[t], o + 1)
+        r0, r1 = bc(tiles[t], o), bc(tiles[t], o + 1)
+        m0, m1 = col == k, col == k + 1
+        r0 = jnp.where(m0, 1.0, jnp.where(m1, 0.0, r0))
+        r1 = jnp.where(m1, 1.0, jnp.where(m0, 0.0, r1))
+        inv = 1.0 / (p * s - q * q)
+        s0 = (s * inv) * r0 - (q * inv) * r1
+        s1 = (p * inv) * r1 - (q * inv) * r0
+        keep = jnp.where(m0 | m1, 0.0, 1.0)
+        new = [x * keep - c0[i] * s0 - c1[i] * s1 for i, x in enumerate(tiles)]
+        new[t] = jnp.where(sub == o, s0, jnp.where(sub == o + 1, s1, new[t]))
+        tiles = new
+    return jnp.concatenate(tiles, axis=0)
+
+def factor_kernel(xrow_ref, xcol_ref, reg_ref, prec_ref, s_ref):
+    nb = xcol_ref.shape[0]
+    lane = lax.broadcasted_iota(jnp.int32, (nb * B, 2 * B), 1)
+    def wide(d):
+        return jnp.where(lane < B, xrow_ref[:, d : d + 1], xrow_ref[:, 4 + d : 5 + d])
+    rows = [wide(d) for d in range(4)]
+    sub = lax.broadcasted_iota(jnp.int32, (B, 2 * B), 0)
+    dcol = lax.broadcasted_iota(jnp.int32, (B, 2 * B), 1) % B
+    for j in range(nb):
+        sq = None
+        for d in range(3):
+            diff = rows[d][j * B :] - xcol_ref[j, d : d + 1]
+            sq = diff * diff if sq is None else sq + diff * diff
+        mask = xcol_ref[j, 3:4]
+        k = jnp.exp(-jnp.sqrt(sq) / 0.35) * rows[3][j * B :] * mask
+        s_ref[j, j * B :] = k
+        s_ref[j, j * B : (j + 1) * B] = k[:B] + jnp.where(sub == dcol, 0.5 * mask + (1.0 - mask), 0.0)
+
+    def step(j, carry):
+        inv = invert_pair(s_ref[j, pl.ds(pl.multiple_of(j * B, B), B)])
+        prec_ref[...] = inv
+        big = diag_pair(inv)
+        for jj in range(nb - 1):
+            @pl.when(j == jj)
+            def _():
+                panel = s_ref[jj, (jj + 1) * B :]
+                w = dot3(panel, big, NN)
+                for i in range(jj + 1, nb):
+                    o = (i - jj - 1) * B
+                    s_ref[i, i * B :] -= dot3(w[o:], diag_pair(panel[o : o + B]), NT)
+                s_ref[jj, (jj + 1) * B :] = w
+        return carry
+    lax.fori_loop(0, nb, step, 0)
+    own = (nb - 1) * B
+    rest = [s_ref[j, own:] for j in range(nb - 1)]
+    for i in range(nb - 2, -1, -1):
+        reg_ref[i] = rest[i]
+        for j in range(i):
+            rest[j] = rest[j] - dot3(rest[i], diag_pair(s_ref[j, i * B : (i + 1) * B]), NN)
+
+def factor(xrow, xcol):
+    nb = xcol.shape[0]
+    return pl.pallas_call(
+        factor_kernel,
+        out_shape=(jax.ShapeDtypeStruct((nb - 1, B, 2 * B), F32), jax.ShapeDtypeStruct((B, 2 * B), F32)),
+        in_specs=[pl.BlockSpec(memory_space=pltpu.VMEM)] * 2,
+        out_specs=(pl.BlockSpec(memory_space=pltpu.VMEM),) * 2,
+        scratch_shapes=[pltpu.VMEM((nb, nb * B, 2 * B), F32)],
+    )(xrow, xcol)
 
 
 def body(coords, field, observed, pair_owner, cond_list, cond_mask):
@@ -110,13 +178,16 @@
     got_x = recv_x[req_owner]
     same_x = got_x[: 2 * NSAME].reshape(2, NSAME, 3, points)
     lift_x = shifted(got_x[2 * NSAME :].reshape(2, cross_covariance, 3, points), "grp", 1)
-    cond_x = (
-        jnp.concatenate([same_x, lift_x], axis=1)
-        .transpose(0, 2, 1, 3)
-        .reshape(2, 3, NCOND * points)
-    )
-    point_mask = jnp.repeat(my_mask, points, axis=1)
-    regress, precision = jax.vmap(factor_block)(own_x, cond_x, point_mask)
+    cond_x = jnp.concatenate([same_x, lift_x], axis=1)
+    all_x = jnp.concatenate([cond_x, own_x[:, None]], axis=1)
+    all_mask = jnp.concatenate([my_mask, jnp.ones((2, 1), jnp.float32)], axis=1)
+    all_mask = jnp.broadcast_to(all_mask[:, :, None, None], (2, NCOND + 1, 1, points))
+    full = jnp.concatenate([all_x, all_mask], axis=2)
+    xrow = full.transpose(1, 3, 0, 2).reshape((NCOND + 1) * points, 8)
+    xcol = full.transpose(1, 2, 0, 3).reshape(NCOND + 1, 4, 2 * points)
+    reg, prec = factor(xrow, xcol)
+    regress = reg.reshape(NCOND, points, 2, points).transpose(2, 0, 3, 1).reshape(2, NCOND * points, points)
+    precision = prec.reshape(points, 2, points).transpose(1, 0, 2)
     state = field.reshape(2, points, out_cols)
     target = observed.reshape(2, points, out_cols)
     slot_mask = my_mask[:, :, None, None]

time: 602 us -> 386 us (0.64)
  other arithmetic: 269 us -> 5.86 us
  Pallas kernels: 0 us -> 43.7 us
  waiting for transfers between devices: 89.3 us -> 126 us
  matrix products: 31.7 us -> 13.5 us
  local copies, waits for them, and re-layouts: 31.7 us -> 19.7 us
    another operation x29 -> x0, other arithmetic: 259 us -> none  [the longest x18 154 us: factor_block(): lower = jnp.linalg.cholesky(kcc)]
    all_gather x2, waiting for transfers between devices: 62.3 us -> 111 us  [body(): piece = lax.all_gather(rounded, 'dev', axis=0, tiled=True)]
    pallas_call x0 -> x1, Pallas kernels: none -> 43.7 us  [factor(): pl.pallas_call(factor_kernel, out_shape=(jax.ShapeDtypeStruct((nb - 1, B,...]
    another operation x21 -> x0, matrix products: 17.5 us -> none  [the longest x6 6.73 us: factor_block(): lower = jnp.linalg.cholesky(kcc)]
    another operation x17 -> x0, local copies, waits for them, and re-layouts: 14.5 us -> none
    all_to_all x1, waiting for transfers between devices: 7.57 us -> 0.01 us  [body(): lax.all_to_all(send_x, 'dev', split_axis=0, concat_axis=0, tiled=True)]
  transfers between devices with their start and end apart: 8 -> 8, of which waited for: 7 -> 6; matrix products, arithmetic and copies ran while one was open for 51% -> 6% of each run, Pallas kernels for 0% -> 11%
where the time goes in v1:
time: 386 us; the launch traced here: 385 us
  blocking collectives  132 us (34%)
  waiting for transfers between devices  126 us (33%)
  Pallas kernels  43.7 us (11%)
  starting transfers between devices  29.8 us (8%)
  local copies, waits for them, and re-layouts  19.7 us (5%)
  between operations  14.6 us (4%)
  matrix products  13.5 us (3%)
  other arithmetic  5.86 us (2%)
    all_to_all x2, blocking collectives, body(): lax.all_to_all(outgo.astype(jnp.bfloat16), 'dev', split_axis=0, concat_ax...  132 us
    all_gather x2, waiting for transfers between devices, body(): piece = lax.all_gather(rounded, 'dev', axis=0, tiled=True)  111 us
    pallas_call x1, Pallas kernels, factor(): pl.pallas_call(factor_kernel, out_shape=(jax.ShapeDtypeStruct((nb - 1, B,...  43.7 us
    all_to_all x1, starting transfers between devices, body(): lax.all_to_all(send_x, 'dev', split_axis=0, concat_axis=0, tiled=True)  15.9 us
    ppermute x5, waiting for transfers between devices, shifted(): return lax.ppermute(block, axis, route)  14.7 us
    ppermute x5, starting transfers between devices, shifted(): return lax.ppermute(block, axis, route)  13.8 us
  transfers between devices with their start and end apart: 8, of which 6 were waited for; matrix products, arithmetic and copies ran while one was open for 6% of the time, Pallas kernels for 11%

profile of v1, /device:TPU:3, one launch (start us, length us, event | category | flops | bytes accessed | tf_op | source)
XLA Modules:
  0.0 385.3 jit_solution(7694225406334854278)
XLA Ops:
  7.2 1.5 convert_element_type.100
  8.8 0.8 select_reduce_fusion
  9.7 0.8 reshape.296
  10.4 0.9 copy.98
  11.4 1.0 copy.100
  12.4 0.6 gather_fusion.5
  13.0 0.6 gather_fusion.3
  13.6 0.6 gather_fusion.2
  14.2 0.6 gather_fusion
  14.8 0.2 and_select_fusion.3
  15.0 0.1 reshape.328
  15.2 0.7 fusion.63
  15.9 2.7 gather_fusion.1
  18.6 0.2 reshape.327
  18.9 0.2 and_select_fusion.1
  19.2 0.1 reshape.352
  19.4 1.2 gather_fusion.4
  20.6 0.2 reshape.351
  21.1 0.1 multiply_add_fusion.1
  21.2 0.7 reshape.382
  21.9 15.9 %all-to-all-start = ((f32[32,1,192]{2,1,0:T(1,128)}), f32[32,1,192]{2,1,0:T(1,128)S(1)}, u32[]{:S(2)}, u32[]{:S(2)}) async-start(f32[32,1,192]{2,1,0:T(1,128)} %reshape.382), calls=%async_computation | async-start | bytes 65536 | tf_op jit(solution)/shard_map/all_to_all | solution.py:177
  38.9 48.3 %all-gather.3.cloned.1.call-done = bf16[64,64,256]{2,1,0:T(8,128)(2,1)} async-done(((bf16[2,64,256]{2,1,0:T(8,128)(2,1)}), bf16[64,64,256]{2,1,0:T(8,128)(2,1)}) %all-gather.3.cloned.1.call-update) | async-done | bytes 2097168 | tf_op jit(solution)/shard_map/all_gather | solution.py:197
  87.1 2.8 fusion.4
  90.1 3.3 collective-permute-start.1
  93.4 0.5 broadcast.200
  93.9 0.7 reduce
  94.7 0.6 gather_fusion.6
  95.3 3.0 collective-permute-start
  98.5 3.3 collective-permute-done
  101.9 0.7 reshape.300.xcol_ref
  102.7 0.9 copy.108.xrow_ref
  103.6 43.7 %shard_map.77 = (f32[8,64,128]{2,1,0:T(8,128)}, f32[64,128]{1,0:T(8,128)}) custom-call(f32[576,8]{1,0:T(8,128)} %copy.108.xrow_ref, f32[9,4,128]{2,1,0:T(4,128)} %reshape.300.xcol_ref), custom_call_target="tpu_custom_call" | custom-call | tf_op jit(solution)/shard_map/pallas_call | solution.py:110
  147.3 0.9 reshape.301
  148.1 1.3 reshape.302
  149.4 0.3 copy.110
  149.7 0.1 reshape.303
  150.1 0.2 copy-done
  150.3 0.9 convolution_subtract_fusion.1
  151.2 0.3 fusion.28
  151.5 1.0 fusion.84
  152.5 0.1 multiply_convert_fusion.1
  152.7 2.2 collective-permute-start.2
  154.9 0.5 fusion.16
  155.5 2.9 collective-permute-done.2
  158.4 0.6 add_convert_fusion.1
  159.0 0.6 copy.116
  159.6 66.4 %all_to_all.15 = bf16[32,64,256]{2,1,0:T(8,128)(2,1)S(1)} all-to-all(bf16[32,64,256]{2,1,0:T(8,128)(2,1)S(1)} %copy.116), channel_id=1, replica_groups=mesh['grp'=16,'dev'=32] {'dev'}, dimensions={0} | all-to-all | bytes 2097152 | tf_op jit(solution)/shard_map/all_to_all | solution.py:226
  226.0 0.7 fusion.12
  226.7 0.7 fusion.79
  227.4 62.9 %all-gather.5.cloned.1.call-done = bf16[64,64,256]{2,1,0:T(8,128)(2,1)} async-done(((bf16[2,64,256]{2,1,0:T(8,128)(2,1)}), bf16[64,64,256]{2,1,0:T(8,128)(2,1)}) %all-gather.5.cloned.1.call-update) | async-done | bytes 2097168 | tf_op jit(solution)/shard_map/all_gather | solution.py:197
  290.3 2.8 fusion.7
  293.2 3.1 collective-permute-start.3
  296.5 5.5 %collective-permute-done.3 = bf16[2,2,64,256]{3,2,1,0:T(8,128)(2,1)S(1)} collective-permute-done((bf16[2,2,64,256]{3,2,1,0:T(8,128)(2,1)S(1)}, bf16[2,2,64,256]{3,2,1,0:T(8,128)(2,1)S(1)}, u32[]{:S(2)}, u32[]{:S(2)}) %collective-permute-start.3) | collective-permute-done | bytes 131104 | tf_op jit(solution)/shard_map/ppermute | solution.py:22
  302.0 0.9 convolution_subtract_fusion
  302.9 0.3 fusion.26
  303.2 1.0 fusion.85
  304.4 2.3 collective-permute-start.4
  306.7 0.5 fusion.14
  307.2 2.9 collective-permute-done.4
  310.1 0.6 add_convert_fusion
  310.7 0.6 copy.124
  311.3 65.8 %all_to_all.16 = bf16[32,64,256]{2,1,0:T(8,128)(2,1)S(1)} all-to-all(bf16[32,64,256]{2,1,0:T(8,128)(2,1)S(1)} %copy.124), channel_id=1, replica_groups=mesh['grp'=16,'dev'=32] {'dev'}, dimensions={0} | all-to-all | bytes 2097152 | tf_op jit(solution)/shard_map/all_to_all | solution.py:226
  377.0 0.7 fusion.10
  377.7 0.7 multiply_add_fusion
  (71 shorter events, 2.8 us)
Async XLA Ops:
  7.2 80.0 %all-gather.3.cloned.1.call-start = ((), (), s32[]{:S(2)}) async-start(), calls=%async_computation.3 | async-start | bytes 2162688 | tf_op jit(solution)/shard_map/all_gather | solution.py:197
  21.9 71.4 %all-to-all-start = ((f32[32,1,192]{2,1,0:T(1,128)}), f32[32,1,192]{2,1,0:T(1,128)S(1)}, u32[]{:S(2)}, u32[]{:S(2)}) async-start(f32[32,1,192]{2,1,0:T(1,128)} %reshape.382), calls=%async_computation | async-start | bytes 65536 | tf_op jit(solution)/shard_map/all_to_all | solution.py:177
  37.9 252.4 %all-gather.5.cloned.1.call-start = ((), (), s32[]{:S(2)}) async-start(), calls=%async_computation.4 | async-start | bytes 2162688 | tf_op jit(solution)/shard_map/all_gather | solution.py:197
  90.1 59.9 %collective-permute-start.1 = (bf16[2,2,64,256]{3,2,1,0:T(8,128)(2,1)S(1)}, bf16[2,2,64,256]{3,2,1,0:T(8,128)(2,1)S(1)}, u32[]{:S(2)}, u32[]{:S(2)}) collective-permute-start(bf16[2,2,64,256]{3,2,1,0:T(8,128)(2,1)S(1)} %bitcast.123), channel_id=1, source_target_pairs={{0,32},{32,64},{64,96},{96,128},{128,160},{160,192},{192,224},{224... | collective-permute-start | bytes 393224 | tf_op jit(solution)/shard_map/ppermute | solution.py:22
  95.3 6.5 %collective-permute-start = (f32[2,2,3,64]{3,1,0,2:T(2,128)S(1)}, f32[2,2,3,64]{3,1,0,2:T(2,128)S(1)}, u32[]{:S(2)}, u32[]{:S(2)}) collective-permute-start(f32[2,2,3,64]{3,1,0,2:T(2,128)S(1)} %bitcast.130), channel_id=1, source_target_pairs={{0,32},{32,64},{64,96},{96,128},{128,160},{160,192},{192,224},{224... | collective-permute-start | bytes 9224 | tf_op jit(solution)/shard_map/ppermute | solution.py:22
  149.4 0.9 copy-start
  152.7 5.7 %collective-permute-start.2 = (bf16[2,2,64,256]{3,2,1,0:T(8,128)(2,1)S(1)}, bf16[2,2,64,256]{3,2,1,0:T(8,128)(2,1)S(1)}, u32[]{:S(2)}, u32[]{:S(2)}) collective-permute-start(bf16[2,2,64,256]{3,2,1,0:T(8,128)(2,1)S(1)} %slice.101), channel_id=1, source_target_pairs={{32,0},{64,32},{96,64},{128,96},{160,128},{192,160},{224,192},{256... | collective-permute-start | bytes 393224 | tf_op jit(solution)/shard_map/ppermute | solution.py:22
  159.6 67.1 %copy-start.1 = (f32[128,256]{1,0:T(8,128)S(1)}, f32[128,256]{1,0:T(8,128)}, u32[]{:S(2)}) copy-start(f32[128,256]{1,0:T(8,128)} %param.8) | copy-start | bytes 393220
  293.2 8.8 %collective-permute-start.3 = (bf16[2,2,64,256]{3,2,1,0:T(8,128)(2,1)S(1)}, bf16[2,2,64,256]{3,2,1,0:T(8,128)(2,1)S(1)}, u32[]{:S(2)}, u32[]{:S(2)}) collective-permute-start(bf16[2,2,64,256]{3,2,1,0:T(8,128)(2,1)S(1)} %bitcast.124), channel_id=1, source_target_pairs={{0,32},{32,64},{64,96},{96,128},{128,160},{160,192},{192,224},{224... | collective-permute-start | bytes 393224 | tf_op jit(solution)/shard_map/ppermute | solution.py:22
  304.4 5.7 %collective-permute-start.4 = (bf16[2,2,64,256]{3,2,1,0:T(8,128)(2,1)S(1)}, bf16[2,2,64,256]{3,2,1,0:T(8,128)(2,1)S(1)}, u32[]{:S(2)}, u32[]{:S(2)}) collective-permute-start(bf16[2,2,64,256]{3,2,1,0:T(8,128)(2,1)S(1)} %slice.105), channel_id=1, source_target_pairs={{32,0},{64,32},{96,64},{128,96},{160,128},{192,160},{224,192},{256... | collective-permute-start | bytes 393224 | tf_op jit(solution)/shard_map/ppermute | solution.py:22
Sparse Core Ops, SparseCore 0:
  10.7 76.4 all-gather.2
  227.5 62.7 all-gather.4

commit v2 on v0

v2 whole, which is shorter than its diff:
```python
import jax
import jax.numpy as jnp
from jax import lax
from jax.experimental import pallas as pl
from jax.experimental.pallas import tpu as pltpu
from jax.sharding import PartitionSpec as P

NCOND = 8
NSAME = 6
NCROSS = NCOND - NSAME
STEPS = 2
HIGH = lax.Precision.HIGHEST
LENGTH_SCALE = 0.35
NUGGET = 0.5
STEP_SIZE = 0.3
MESH = pl.DeviceIdType.MESH
F32 = jnp.float32
BF16 = jnp.bfloat16
B = 64
NB = NCOND + 1
SLOTS = 2 * NCOND
FWD = 2 * NSAME
NFWD = 2 * NCROSS
NN = ((1,), (0,))
NT = ((1,), (1,))

MASK = SLOTS
HALF = MASK + SLOTS
SEL = 40


def offsets(chips):
    give = SEL + 4 * chips
    take = give + chips
    return give, take, take + 2 * chips


def dot(a, b, dims):
    return lax.dot_general(a, b, (dims, ((), ())), precision=HIGH, preferred_element_type=F32)


def table_kernel(owner_ref, list_ref, mask_ref, out_ref):
    members = owner_ref.shape[1]
    chips = members // 2
    give, take, size = offsets(chips)
    base = lax.axis_index("grp") * 2 * members
    me = lax.axis_index("dev")
    core = me % 2

    def clear(i, carry):
        out_ref[SEL + i] = SLOTS
        return carry

    lax.fori_loop(0, 5 * chips, clear, 0)

    def zero(i, carry):
        out_ref[take + i] = 0
        return carry

    lax.fori_loop(0, 2 * chips, zero, 0)
    for partner in (False, True):
        device = me + 1 - 2 * core if partner else me

        def find(group):
            def look(i, found):
                return found + jnp.where(owner_ref[group, i] == device, i, 0)

            return lax.fori_loop(0, members, look, 0)

        pair, next_pair = find(0), find(1)
        for half in range(2):
            for slot in range(NCOND):
                cross = slot >= NSAME
                group, row = (1, 2 * next_pair + half) if cross else (0, 2 * pair + half)
                block = list_ref[group, row, slot]
                used = mask_ref[group, row, slot]
                index = FWD + half * NCROSS + slot - NSAME if cross else half * NSAME + slot
                where = jnp.minimum(jnp.maximum((block - base) // 2, 0), members - 1)
                owner = owner_ref[0, where]
                side = block % 2
                if partner:

                    @pl.when((used == 1) & (owner % 2 == core))
                    def _():
                        out_ref[take + owner - core + side] = 1
                else:
                    out_ref[index] = 2 * owner + side
                    out_ref[MASK + half * NCOND + slot] = mask_ref[0, 2 * pair + half, slot]
                    if cross:
                        out_ref[HALF + half * NCROSS + slot - NSAME] = list_ref[0, 2 * pair + half, slot] % 2

                    @pl.when(used == 1)
                    def _():
                        out_ref[SEL + 2 * owner + side] = index

                    @pl.when((used == 1) & (owner % 2 != core))
                    def _():
                        out_ref[give + owner // 2] = index


def diag_pair(block):
    both = jnp.concatenate([block, block], axis=0)
    row = lax.broadcasted_iota(jnp.int32, (2 * B, 2 * B), 0)
    lane = lax.broadcasted_iota(jnp.int32, (2 * B, 2 * B), 1)
    return jnp.where((row < B) == (lane < B), both, 0.0)


def inverse2(p, q, s):
    inv = 1.0 / (p * s - q * q)
    a, b, c = s * inv, q * inv, p * inv
    return lambda x, y: (a * x - b * y, c * y - b * x)


def invert_pair(a):
    lane = lax.broadcasted_iota(jnp.int32, (B, 2 * B), 1)
    sub = lax.broadcasted_iota(jnp.int32, (B, 2 * B), 0)
    col = jnp.where(lane < B, lane, lane - B)
    for k in range(0, B, 4):
        c = [
            jnp.where(
                lane < B,
                jnp.broadcast_to(a[:, i : i + 1], (B, 2 * B)),
                jnp.broadcast_to(a[:, B + i : B + i + 1], (B, 2 * B)),
            )
            for i in range(k, k + 4)
        ]
        pivot = (col >= k) & (col < k + 4)

        def g(i, j):
            return c[j][k + i : k + i + 1]

        r = [
            jnp.where(col[:1] == k + i, 1.0, jnp.where(pivot[:1], 0.0, a[k + i : k + i + 1]))
            for i in range(4)
        ]
        first = inverse2(g(0, 0), g(1, 0), g(1, 1))
        v0, v1 = first(r[0], r[1])
        g02, g12 = first(g(0, 2), g(1, 2))
        g03, g13 = first(g(0, 3), g(1, 3))
        second = inverse2(
            g(2, 2) - (g(0, 2) * g02 + g(1, 2) * g12),
            g(3, 2) - (g(0, 3) * g02 + g(1, 3) * g12),
            g(3, 3) - (g(0, 3) * g03 + g(1, 3) * g13),
        )
        s2, s3 = second(r[2] - (g(0, 2) * v0 + g(1, 2) * v1), r[3] - (g(0, 3) * v0 + g(1, 3) * v1))
        s0 = v0 - (g02 * s2 + g03 * s3)
        s1 = v1 - (g12 * s2 + g13 * s3)
        a = jnp.where(pivot, 0.0, a) - (c[0] * s0 + c[1] * s1) - (c[2] * s2 + c[3] * s3)
        for i, solved in enumerate((s0, s1, s2, s3)):
            a = jnp.where(sub == k + i, solved, a)
    return a


def main_kernel(
    tab, x_ref, f_ref, y_ref, field_ref, grad_ref,
    cx, fxs, fx, xcol, xrow, s_ref, prec_ref, reg_ref, regt_ref, state, scaled,
    everyone, fwd, got, back, home, give_buf, take_buf, out_buf, in_buf,
    cs, cr, cps, cpr, xfs, xfr, gs, gr, ps, pr, fs, fr, bs, br, vs, vr, rs, rr,
):
    members = cx.shape[0]
    chips = members // 2
    hops = chips // 2
    give, take, size = offsets(chips)
    groups = lax.axis_size("grp")
    group = lax.axis_index("grp")
    me = lax.axis_index("dev")
    core = me % 2
    chip = me // 2

    def around(step):
        return (chip + step + chips) % chips

    right = (group, 2 * around(1) + core)
    left = (group, 2 * around(-1) + core)
    toward = (right, left)
    sign = (1, -1)
    partner = (group, me + 1 - 2 * core)
    after = ((group + 1) % groups, me)
    before = ((group + groups - 1) % groups, me)

    barrier = pltpu.get_barrier_semaphore()
    for peer in (right, left, partner, after, before):
        pl.semaphore_signal(barrier, inc=1, device_id=peer, device_id_type=MESH)
    pl.semaphore_wait(barrier, 5)

    def copy(src, dst, send, recv, peer):
        return pltpu.make_async_remote_copy(
            src_ref=src, dst_ref=dst, send_sem=send, recv_sem=recv, device_id=peer, device_id_type=MESH
        )

    def coord_hop(d, hop):
        src = x_ref if hop == 1 else cx.at[2 * around(-sign[d] * (hop - 1)) + core]
        dst = cx.at[2 * around(-sign[d] * (hop - 1)) + core]
        return copy(src, dst, cs.at[d, hop - 1], cr.at[d, hop - 1], toward[d])

    def coord_got(d, hop):
        ref = cx.at[2 * around(-sign[d] * hop) + core]
        return copy(ref, ref, cs.at[d, hop - 1], cr.at[d, hop - 1], toward[d])

    def coord_pass(d, hop):
        ref = cx.at[2 * around(-sign[d] * hop) + core]
        return copy(ref, ref, cps.at[d, hop], cpr.at[d, hop], partner)

    def coord_passed(d, hop):
        ref = cx.at[2 * around(-sign[d] * hop) + 1 - core]
        return copy(ref, ref, cps.at[d, hop], cpr.at[d, hop], partner)

    def ways(hop):
        return (0, 1) if hop < hops else (0,)

    for d in ways(1):
        coord_hop(d, 1).start()
    copy(x_ref, cx.at[me], cps.at[0, 0], cpr.at[0, 0], partner).start()
    cx[me] = x_ref[...]

    def gather_send(st, d, hop, half):
        ref = everyone.at[st, 4 * around(-sign[d] * (hop - 1)) + 2 * core + half]
        return copy(ref, ref, gs.at[d, hop - 1, half], gr.at[d, hop - 1, half], toward[d])

    def gather_got(st, d, hop, half):
        ref = everyone.at[st, 4 * around(-sign[d] * hop) + 2 * core + half]
        return copy(ref, ref, gs.at[d, hop - 1, half], gr.at[d, hop - 1, half], toward[d])

    def gather_pass(st, d, hop, half):
        ref = everyone.at[st, 4 * around(-sign[d] * hop) + 2 * core + half]
        return copy(ref, ref, ps.at[d, hop, half], pr.at[d, hop, half], partner)

    def gather_passed(st, d, hop, half):
        ref = everyone.at[st, 4 * around(-sign[d] * hop) + 2 * (1 - core) + half]
        return copy(ref, ref, ps.at[d, hop, half], pr.at[d, hop, half], partner)

    def lanes(hop):
        return [(d, half) for half in range(2) for d in range(2) if hop < hops or d == half]

    def gather_begin(st):
        for half in range(2):
            everyone[st, 2 * me + half] = state[half].astype(BF16)
        for d, half in lanes(1):
            gather_send(st, d, 1, half).start()
        for half in range(2):
            gather_pass(st, 0, 0, half).start()

    def gather_next(st, hop):
        for d, half in lanes(hop):
            gather_got(st, d, hop, half).wait_recv()
            if hop < hops and (d, half) in lanes(hop + 1):
                gather_send(st, d, hop + 1, half).start()
            gather_pass(st, d, hop, half).start()

    def gather_end(st):
        for half in range(2):
            gather_passed(st, 0, 0, half).wait()
        for hop in range(1, hops + 1):
            for d, half in lanes(hop):
                gather_passed(st, d, hop, half).wait()
                gather_send(st, d, hop, half).wait_send()

    def forward(st):
        for i in range(NFWD):
            fwd[st, i] = everyone[st, tab[FWD + i]]
            copy(fwd.at[st, i], got.at[st, i], fs.at[i], fr.at[i], after).start()

    def forwarded(st):
        for i in range(NFWD):
            copy(fwd.at[st, i], got.at[st, i], fs.at[i], fr.at[i], after).wait()

    state[...] = f_ref[...]
    for hop in range(1, hops + 1):
        for d in ways(hop):
            coord_got(d, hop).wait_recv()
            if hop < hops and d in ways(hop + 1):
                coord_hop(d, hop + 1).start()
            coord_pass(d, hop).start()
    coord_passed(0, 0).wait()
    for hop in range(1, hops + 1):
        for d in ways(hop):
            coord_passed(d, hop).wait()
            coord_hop(d, hop).wait_send()
    for i in range(NFWD):
        fxs[i] = cx[tab[FWD + i] // 2]
        copy(fxs.at[i], fx.at[i], xfs.at[i], xfr.at[i], after).start()
    gather_begin(0)
    for i in range(NFWD):
        copy(fxs.at[i], fx.at[i], xfs.at[i], xfr.at[i], after).wait()

    lane8 = lax.broadcasted_iota(jnp.int32, (8, 2 * B), 1)
    sub8 = lax.broadcasted_iota(jnp.int32, (8, 2 * B), 0)
    lane = lax.broadcasted_iota(jnp.int32, (B, 2 * B), 1)
    sub = lax.broadcasted_iota(jnp.int32, (B, 2 * B), 0)
    point = jnp.where(lane < B, lane, lane - B)

    def mask(half, slot):
        return tab[MASK + half * NCOND + slot].astype(F32)

    for j in range(NB):
        if j == NCOND:
            placed = jnp.where(sub8 == 3, 1.0, x_ref[...])
        else:
            sides = []
            for half in range(2):
                if j < NSAME:
                    row = tab[half * NSAME + j]
                    found, side = cx[row // 2], row % 2
                else:
                    i = half * NCROSS + j - NSAME
                    found, side = fx[i], tab[HALF + i]
                turned = jnp.concatenate([found[:, B:], found[:, :B]], axis=1)
                same = (side == half).astype(F32)
                sides.append(found * same + turned * (1.0 - same))
            placed = jnp.where(lane8 < B, sides[0], sides[1])
            weights = jnp.where(lane8 < B, mask(0, j), mask(1, j))
            placed = jnp.where(sub8 == 3, weights, placed)
        xcol[j] = placed
        standing = placed.T
        for d in range(4):
            xrow[d, j * B : (j + 1) * B] = jnp.where(
                lane < B, standing[:B, d : d + 1], standing[B:, d : d + 1]
            )
    for j in range(NB):
        sq = None
        for d in range(3):
            diff = xrow[d, j * B :] - xcol[j, d : d + 1]
            sq = diff * diff if sq is None else sq + diff * diff
        weights = xcol[j, 3:4]
        s_ref[j, j * B :] = jnp.exp(-jnp.sqrt(sq) / LENGTH_SCALE) * xrow[3, j * B :] * weights
        s_ref[j, j * B : (j + 1) * B] += jnp.where(
            sub == point, NUGGET * weights + (1.0 - weights), 0.0
        )

    def eliminate(j, carry):
        inv = invert_pair(s_ref[j, pl.ds(pl.multiple_of(j * B, B), B)])
        prec_ref[...] = inv
        big = diag_pair(inv)
        for jj in range(NCOND):

            @pl.when(j == jj)
            def _():
                if 1 <= jj <= hops:
                    gather_next(0, jj)
                panel = s_ref[jj, (jj + 1) * B :]
                w = dot(panel, big, NN)
                for i in range(jj + 1, NB):
                    o = (i - jj - 1) * B
                    s_ref[i, i * B :] -= dot(w[o:], diag_pair(panel[o : o + B]), NT)
                s_ref[jj, (jj + 1) * B :] = w

        return carry

    lax.fori_loop(0, NB, eliminate, 0)
    for hop in range(NCOND, hops + 1):
        gather_next(0, hop)
    gather_end(0)
    forward(0)
    own = NCOND * B
    rest = [s_ref[j, own:] for j in range(NCOND)]
    for i in range(NCOND - 1, -1, -1):
        turned = rest[i].T
        for half in range(2):
            reg_ref[half, :, i * B : (i + 1) * B] = rest[i][:, half * B : (half + 1) * B]
            regt_ref[half, i * B : (i + 1) * B] = turned[half * B : (half + 1) * B]
        for j in range(i):
            rest[j] = rest[j] - dot(rest[i], diag_pair(s_ref[j, i * B : (i + 1) * B]), NN)

    for st in range(STEPS):
        if st:
            gather_begin(st)
            for hop in range(1, hops + 1):
                gather_next(st, hop)
            gather_end(st)
            forward(st)
        forwarded(st)
        for half in range(2):
            cond = [
                everyone[st, tab[half * NSAME + s]].astype(F32) * mask(half, s) for s in range(NSAME)
            ] + [
                got[st, half * NCROSS + s].astype(F32) * mask(half, NSAME + s) for s in range(NCROSS)
            ]
            resid = state[half] - dot(reg_ref[half], jnp.concatenate(cond, axis=0), NN)
            solved = dot(prec_ref[:, half * B : (half + 1) * B], resid, NN)
            scaled[half] = solved
            terms = dot(regt_ref[half], solved, NN)
            for s in range(NCOND):
                term = (terms[s * B : (s + 1) * B] * mask(half, s)).astype(BF16)
                if s < NSAME:
                    back[st, half * NSAME + s] = term
                else:
                    home[st, half * NCROSS + s - NSAME] = term
        for i in range(NFWD):
            copy(home.at[st, i], back.at[st, FWD + i], bs.at[i], br.at[i], before).start()
        back[st, SLOTS] = jnp.zeros((B, back.shape[3]), BF16)
        for i in range(NFWD):
            copy(home.at[st, i], back.at[st, FWD + i], bs.at[i], br.at[i], before).wait()

        order = [around(hops)]
        for step in range(hops - 1, 0, -1):
            order += [around(step), around(-step)]
        order.append(chip)

        def given(n):
            ref = give_buf.at[st, n]
            return copy(ref, take_buf.at[st, n], vs.at[n], vr.at[n], partner)

        for n, dest in enumerate(order):
            give_buf[st, n] = back[st, tab[give + dest]]
            given(n).start()

        def owed(n, half):
            dest = order[n]
            mine = back[st, tab[SEL + 4 * dest + 2 * core + half]].astype(F32)
            return mine + take_buf[st, n].astype(F32) * tab[take + 2 * dest + half].astype(F32)

        def carried(d, hop, half):
            return copy(
                out_buf.at[st, d, hop - 1, half], in_buf.at[st, d, hop - 1, half],
                rs.at[d, hop - 1, half], rr.at[d, hop - 1, half], toward[d],
            )

        def starts(hop):
            return [(d, half) for half in range(2) for d in range(2) if hop > 1 or d == half]

        given(0).wait_recv()
        for hop in range(1, hops + 1):
            if hop > 1:
                for d in range(2):
                    given(2 * hop - 3 + d).wait_recv()
            for d, half in starts(hop):
                total = owed(0 if hop == 1 else 2 * hop - 3 + d, half)
                if hop > 1 and (d, half) in starts(hop - 1):
                    carried(d, hop - 1, half).wait_recv()
                    total = total + in_buf[st, d, hop - 2, half].astype(F32)
                out_buf[st, d, hop - 1, half] = total.astype(BF16)
                carried(d, hop, half).start()
        last = 2 * hops - 1
        given(last).wait_recv()
        for half in range(2):
            incoming = owed(last, half)
            for d in range(2):
                if (d, half) in starts(hops):
                    carried(d, hops, half).wait_recv()
                    incoming = incoming + in_buf[st, d, hops - 1, half].astype(F32)
            now = state[half]
            grad = jnp.tanh(y_ref[half] - now) - (scaled[half] - incoming)
            state[half] = now + STEP_SIZE * grad
            grad_ref[half] = grad
        for n in range(2 * hops):
            given(n).wait_send()
        for hop in range(1, hops + 1):
            for d, half in starts(hop):
                carried(d, hop, half).wait_send()
    field_ref[...] = state[...]


def body(coords, field, observed, pair_owner, cond_list, cond_mask):
    groups = lax.axis_size("grp")
    members = lax.axis_size("dev")
    chips = members // 2
    hops = chips // 2
    group = lax.axis_index("grp")
    following = jnp.minimum(group + 1, groups - 1)
    has_next = (group + 1 < groups).astype(jnp.int32)
    cols = field.shape[1]
    lists = cond_list.reshape(groups, 2 * members, NCOND)
    masks = cond_mask.reshape(groups, 2 * members, NCOND)

    def both(array):
        return jnp.stack([array[group], array[following]])

    masks = both(masks) * jnp.stack([jnp.int32(1), has_next])[:, None, None]
    size = offsets(chips)[2]
    smem = pl.BlockSpec(memory_space=pltpu.SMEM)
    vmem = pl.BlockSpec(memory_space=pltpu.VMEM)
    table = pl.pallas_call(
        table_kernel,
        out_shape=jax.ShapeDtypeStruct((size,), jnp.int32),
        in_specs=[smem] * 3,
        out_specs=smem,
        name="tables",
    )(both(pair_owner), both(lists), masks)
    x = jnp.pad(coords, ((0, 5), (0, 0)))
    sem = pltpu.SemaphoreType.DMA
    block = (B, cols)
    shape = (2, B, cols)
    out = pl.pallas_call(
        main_kernel,
        out_shape=(jax.ShapeDtypeStruct(shape, F32), jax.ShapeDtypeStruct(shape, F32)),
        in_specs=[smem, vmem, vmem, vmem],
        out_specs=(vmem, vmem),
        scratch_shapes=[
            pltpu.VMEM((members, 8, 2 * B), F32),
            pltpu.VMEM((NFWD, 8, 2 * B), F32),
            pltpu.VMEM((NFWD, 8, 2 * B), F32),
            pltpu.VMEM((NB, 8, 2 * B), F32),
            pltpu.VMEM((4, NB * B, 2 * B), F32),
            pltpu.VMEM((NB, NB * B, 2 * B), F32),
            pltpu.VMEM((B, 2 * B), F32),
            pltpu.VMEM((2, B, NCOND * B), F32),
            pltpu.VMEM((2, NCOND * B, B), F32),
            pltpu.VMEM(shape, F32),
            pltpu.VMEM(shape, F32),
            pltpu.VMEM((STEPS, 2 * members) + block, BF16),
            pltpu.VMEM((STEPS, NFWD) + block, BF16),
            pltpu.VMEM((STEPS, NFWD) + block, BF16),
            pltpu.VMEM((STEPS, SLOTS + 1) + block, BF16),
            pltpu.VMEM((STEPS, NFWD) + block, BF16),
            pltpu.VMEM((STEPS, chips) + block, BF16),
            pltpu.VMEM((STEPS, chips) + block, BF16),
            pltpu.VMEM((STEPS, 2, hops, 2) + block, BF16),
            pltpu.VMEM((STEPS, 2, hops, 2) + block, BF16),
            sem((2, hops)), sem((2, hops)),
            sem((2, hops + 1)), sem((2, hops + 1)),
            sem((NFWD,)), sem((NFWD,)),
            sem((2, hops, 2)), sem((2, hops, 2)),
            sem((2, hops + 1, 2)), sem((2, hops + 1, 2)),
            sem((NFWD,)), sem((NFWD,)),
            sem((NFWD,)), sem((NFWD,)),
            sem((chips,)), sem((chips,)),
            sem((2, hops, 2)), sem((2, hops, 2)),
        ],
        compiler_params=pltpu.CompilerParams(
            collective_id=0, has_side_effects=True, vmem_limit_bytes=48 * 1024 * 1024
        ),
        name="vecchia",
    )(table, x, field.reshape(shape), observed.reshape(shape))
    return tuple(array.reshape(2 * B, cols) for array in out)


def solution(mesh):
    placed = (
        P(None, ("grp", "dev")),
        P(("grp", "dev"), None),
        P(("grp", "dev"), None),
        P(),
        P(),
        P(),
    )
    return jax.shard_map(
        body,
        mesh=mesh,
        in_specs=placed,
        out_specs=(P(("grp", "dev"), None), P(("grp", "dev"), None)),
        check_vma=False,
    )
```

time: 602 us -> 203 us (0.34)
  the two profiles are of different devices: /device:TPU:3 before, /device:TPU:62 now
where the time goes in v2:
time: 203 us; the launch traced here: 202 us
  Pallas kernels  196 us (97%)
  local copies, waits for them, and re-layouts  3.91 us (2%)
    pallas_call x1, Pallas kernels, body(): pl.pallas_call(main_kernel, out_shape=(jax.ShapeDtypeStruct(shape, F32),...  190 us
    pallas_call x1, Pallas kernels, body(): pl.pallas_call(table_kernel, out_shape=jax.ShapeDtypeStruct((size,), jnp....  6.24 us

profile of v2, /device:TPU:62, one launch (start us, length us, event | category | flops | bytes accessed | tf_op | source)
XLA Modules:
  0.0 202.4 jit_solution(6318833084632962943)
XLA Ops:
  0.6 0.0 copy-start.3
  0.6 1.0 copy.22
  1.6 0.0 copy-done.3
  1.6 0.2 copy.23
  1.9 0.1 add_convert_fusion
  1.9 0.7 add_multiply_fusion.mask_ref
  2.6 0.0 copy-start
  2.6 0.0 copy-start.1
  2.6 0.6 pad_add_fusion.list_ref
  3.3 0.8 constant_dynamic-slice_fusion.5
  4.0 0.6 pad_add_fusion.1.owner_ref
  4.6 0.0 copy-start.4
  4.6 6.2 %tables.1.tab = s32[152]{0:T(256)} custom-call(s32[2,32]{1,0:T(2,128)} %pad_add_fusion.1.owner_ref, s32[2,64,8]{2,1,0:T(8,128)} %pad_add_fusion.list_ref, s32[2,64,8]{2,1,0:T(8,128)} %add_multiply_fusion.mask_ref), custom_call_target="tpu_custom_call" | custom-call | tf_op jit(solution)/shard_map/tables/pallas_call | solution.py:472
  10.9 0.0 copy-done.4
  10.9 0.0 copy-start.2
  10.9 0.0 copy-done
  10.9 0.0 copy-done.1
  10.9 0.6 copy-done.2
  11.6 189.5 %vecchia.1 = (f32[2,64,256]{2,1,0:T(8,128)S(1)}, f32[2,64,256]{2,1,0:T(8,128)S(1)}) custom-call(s32[152]{0:T(256)S(1)} %copy-done.2, f32[8,128]{1,0:T(8,128)S(1)} %pad.4.x_ref, f32[2,64,256]{2,1,0:T(8,128)S(1)} %bitcast.7, f32[2,64,256]{2,1,0:T(8,128)S(1)} %bitcast.8), custom_call_target="tpu_custom_call" | custom-call | tf_op jit(solution)/shard_map/vecchia/pallas_call | solution.py:483
  201.1 0.7 copy.26
  201.8 0.7 copy.27
  (2 shorter events, 0.0 us)
Async XLA Ops:
  0.6 1.0 copy-start.3
  2.6 8.3 %copy-start = (f32[128,256]{1,0:T(8,128)S(1)}, f32[128,256]{1,0:T(8,128)}, u32[]{:S(2)}) copy-start(f32[128,256]{1,0:T(8,128)} %param.7) | copy-start | bytes 393220
  2.6 8.3 %copy-start.1 = (f32[128,256]{1,0:T(8,128)S(1)}, f32[128,256]{1,0:T(8,128)}, u32[]{:S(2)}) copy-start(f32[128,256]{1,0:T(8,128)} %param.8) | copy-start | bytes 393220
  4.6 6.2 %copy-start.4 = (f32[3,128]{1,0:T(4,128)S(1)}, f32[3,128]{1,0:T(4,128)}, u32[]{:S(2)}) copy-start(f32[3,128]{1,0:T(4,128)} %param.6) | copy-start | bytes 4612
  10.9 0.7 copy-start.2

commit v3 on v2

v3 whole, which is shorter than its diff:
```python
import jax
import jax.numpy as jnp
from jax import lax
from jax.experimental import pallas as pl
from jax.experimental.pallas import tpu as pltpu
from jax.sharding import PartitionSpec as P

NCOND = 8
NSAME = 6
NCROSS = NCOND - NSAME
STEPS = 2
HIGH = lax.Precision.HIGHEST
LENGTH_SCALE = 0.35
NUGGET = 0.5
STEP_SIZE = 0.3
MESH = pl.DeviceIdType.MESH
F32 = jnp.float32
BF16 = jnp.bfloat16
B = 64
NB = NCOND + 1
SLOTS = 2 * NCOND
FWD = 2 * NSAME
NFWD = 2 * NCROSS
NN = ((1,), (0,))
NT = ((1,), (1,))

MASK = SLOTS
HALF = MASK + SLOTS
SEL = 40


def offsets(chips):
    give = SEL + 4 * chips
    take = give + chips
    return give, take, take + 2 * chips


def dot(a, b, dims):
    return lax.dot_general(a, b, (dims, ((), ())), precision=HIGH, preferred_element_type=F32)


def plain(a, b):
    return jnp.dot(a, b, preferred_element_type=F32)


def split(a):
    high = a.astype(BF16)
    return high, (a - high.astype(F32)).astype(BF16)


def diag_pair(block):
    both = jnp.concatenate([block, block], axis=0)
    row = lax.broadcasted_iota(jnp.int32, (2 * B, 2 * B), 0)
    lane = lax.broadcasted_iota(jnp.int32, (2 * B, 2 * B), 1)
    return jnp.where((row < B) == (lane < B), both, 0.0)


def inverse2(p, q, s):
    inv = 1.0 / (p * s - q * q)
    a, b, c = s * inv, q * inv, p * inv
    return lambda x, y: (a * x - b * y, c * y - b * x)


def invert_pair(a):
    lane = lax.broadcasted_iota(jnp.int32, (B, 2 * B), 1)
    col = jnp.where(lane < B, lane, lane - B)
    col8 = col[:8]
    sub8 = lax.broadcasted_iota(jnp.int32, (8, 2 * B), 0)

    def row(x, i):
        return jnp.broadcast_to(x[i : i + 1], (8, 2 * B))

    def tall(x):
        return jnp.concatenate([x] * (B // 8), axis=0)

    for k in range(0, B, 4):
        c = [
            jnp.where(
                lane < B,
                jnp.broadcast_to(a[:, i : i + 1], (B, 2 * B)),
                jnp.broadcast_to(a[:, B + i : B + i + 1], (B, 2 * B)),
            )
            for i in range(k, k + 4)
        ]
        entry = {(i, j): row(c[j], k + i) for i in range(4) for j in range(i + 1)}

        def g(i, j):
            return entry[max(i, j), min(i, j)]

        pivot = (col >= k) & (col < k + 4)
        r = [
            jnp.where(col8 == k + i, 1.0, jnp.where(pivot[:8], 0.0, row(a, k + i))) for i in range(4)
        ]
        first = inverse2(g(0, 0), g(1, 0), g(1, 1))
        g02, g12 = first(g(0, 2), g(1, 2))
        g03, g13 = first(g(0, 3), g(1, 3))
        second = inverse2(
            g(2, 2) - (g(0, 2) * g02 + g(1, 2) * g12),
            g(3, 2) - (g(0, 3) * g02 + g(1, 3) * g12),
            g(3, 3) - (g(0, 3) * g03 + g(1, 3) * g13),
        )
        v0, v1 = first(r[0], r[1])
        s2, s3 = second(r[2] - (g(0, 2) * v0 + g(1, 2) * v1), r[3] - (g(0, 3) * v0 + g(1, 3) * v1))
        s0 = v0 - (g02 * s2 + g03 * s3)
        s1 = v1 - (g12 * s2 + g13 * s3)
        a = (
            jnp.where(pivot, 0.0, a)
            - (c[0] * tall(s0) + c[1] * tall(s1))
            - (c[2] * tall(s2) + c[3] * tall(s3))
        )
        top = k // 8 * 8
        rows = a[top : top + 8]
        for i, solved in enumerate((s0, s1, s2, s3)):
            rows = jnp.where(sub8 == k - top + i, solved, rows)
        a = jnp.concatenate([p for p in (a[:top], rows, a[top + 8 :]) if p.shape[0]], axis=0)
    return a


def main_kernel(
    owner_ref, list_ref, mask_ref, x_ref, f_ref, y_ref, field_ref, grad_ref, tab, keys,
    cx, fxs, fx, xcol, xrow, s_ref, prec_ref, reg_ref, regt_ref, state, scaled,
    everyone, fwd, got, back, home, give_buf, take_buf, out_buf, in_buf,
    cs, cr, cps, cpr, xfs, xfr, gs, gr, ps, pr, fs, fr, bs, br, vs, vr, rs, rr,
):
    members = cx.shape[0]
    chips = members // 2
    hops = chips // 2
    give, take, size = offsets(chips)
    groups = lax.axis_size("grp")
    group = lax.axis_index("grp")
    me = lax.axis_index("dev")
    core = me % 2
    chip = me // 2

    def around(step):
        return (chip + step + chips) % chips

    def along(step, side):
        return (group, 2 * around(step) + side)

    sign = (1, -1)
    partner = along(0, 1 - core)
    after = ((group + 1) % groups, me)
    before = ((group + groups - 1) % groups, me)
    reach = min(4, hops)

    barrier = pltpu.get_barrier_semaphore()
    near = [along(way * step, side) for step in range(1, reach + 1) for way in sign for side in range(2)]
    for peer in near + [partner, after, before]:
        pl.semaphore_signal(barrier, inc=1, device_id=peer, device_id_type=MESH)
    pl.semaphore_wait(barrier, len(near) + 3)

    def copy(src, dst, send, recv, peer):
        return pltpu.make_async_remote_copy(
            src_ref=src, dst_ref=dst, send_sem=send, recv_sem=recv, device_id=peer, device_id_type=MESH
        )

    def coord_send(d, dist, side):
        start = reach * ((dist - 1) // reach)
        place = 2 * around(-sign[d] * start) + core
        src = cx.at[place] if start else x_ref
        return copy(
            src, cx.at[place], cs.at[d, dist - 1, side], cr.at[d, dist - 1, core],
            along(sign[d] * (dist - start), side),
        )

    def coord_got(d, dist, side):
        ref = cx.at[2 * around(-sign[d] * dist) + side]
        return copy(ref, ref, cs.at[d, dist - 1, side], cr.at[d, dist - 1, side], partner)

    paths = [(d, dist) for dist in range(hops, 0, -1) for d in range(2) if dist < hops or d == 0]
    for d, dist in paths:
        if dist <= reach:
            for side in range(2):
                coord_send(d, dist, side).start()
    copy(x_ref, cx.at[me], cps.at[0], cpr.at[0], partner).start()
    cx[me] = x_ref[...]

    base = group * 2 * members

    def find(which, device):
        def look(i, found):
            return jnp.where(owner_ref[which, i] == device, i, found)

        return lax.fori_loop(0, members, look, 0)

    for other in range(2):
        device = me + 1 - 2 * core if other else me
        pair, next_pair = find(0, device), find(1, device)
        for half in range(2):
            for slot in range(NCOND):
                which, row = (0, 2 * pair + half) if slot < NSAME else (1, 2 * next_pair + half)
                block = list_ref[which, slot, row]
                used = mask_ref[which, slot, row]
                spot = jnp.minimum(jnp.maximum((block - base) // 2, 0), members - 1)
                stored = 2 * owner_ref[0, spot] + block % 2
                index = half * NSAME + slot if slot < NSAME else FWD + half * NCROSS + slot - NSAME
                keys[other * SLOTS + index] = jnp.where(used == 1, stored, -1)
                if not other:
                    tab[index] = stored
                    tab[MASK + half * NCOND + slot] = mask_ref[0, slot, 2 * pair + half]
                    if slot >= NSAME:
                        tab[HALF + half * NCROSS + slot - NSAME] = list_ref[0, slot, 2 * pair + half] % 2

    def owe(i, carry):
        found = SLOTS
        for r in range(SLOTS):
            found = jnp.where(keys[r] == i, r, found)
        tab[SEL + i] = found
        return carry

    lax.fori_loop(0, 2 * members, owe, 0)

    def trade(i, carry):
        far = SEL + 4 * i + 2 * (1 - core)
        tab[give + i] = jnp.minimum(tab[far], tab[far + 1])
        for half in range(2):
            hit = 0
            for r in range(SLOTS):
                hit = jnp.where(keys[SLOTS + r] == 4 * i + 2 * core + half, 1, hit)
            tab[take + 2 * i + half] = hit
        return carry

    lax.fori_loop(0, chips, trade, 0)

    def gather_send(st, d, hop, half):
        start = 2 * ((hop - 1) // 2)
        ref = everyone.at[st, 4 * around(-sign[d] * start) + 2 * core + half]
        return copy(
            ref, ref, gs.at[d, hop - 1, half], gr.at[d, hop - 1, half],
            along(sign[d] * (hop - start), core),
        )

    def gather_got(st, d, hop, half):
        ref = everyone.at[st, 4 * around(-sign[d] * hop) + 2 * core + half]
        return copy(ref, ref, gs.at[d, hop - 1, half], gr.at[d, hop - 1, half], partner)

    def gather_pass(st, d, hop, half):
        ref = everyone.at[st, 4 * around(-sign[d] * hop) + 2 * core + half]
        return copy(ref, ref, ps.at[d, hop, half], pr.at[d, hop, half], partner)

    def gather_passed(st, d, hop, half):
        ref = everyone.at[st, 4 * around(-sign[d] * hop) + 2 * (1 - core) + half]
        return copy(ref, ref, ps.at[d, hop, half], pr.at[d, hop, half], partner)

    def lanes(hop):
        return [(d, half) for half in range(2) for d in range(2) if hop < hops or d == half]

    def gather_begin(st):
        for half in range(2):
            everyone[st, 2 * me + half] = state[half].astype(BF16)
        for hop in (2, 1):
            for d, half in lanes(hop):
                gather_send(st, d, hop, half).start()
        for half in range(2):
            gather_pass(st, 0, 0, half).start()

    def gather_next(st, hop):
        for d, half in lanes(hop):
            gather_got(st, d, hop, half).wait_recv()
            if hop < hops:
                if (d, half) in lanes(hop + 2):
                    gather_send(st, d, hop + 2, half).start()
                gather_send(st, d, hop + 1, half).start()
            gather_pass(st, d, hop, half).start()
        for d, half in lanes(hop - 1):
            gather_got(st, d, hop - 1, half).wait_recv()
            gather_pass(st, d, hop - 1, half).start()

    def gather_end(st):
        for half in range(2):
            gather_passed(st, 0, 0, half).wait()
        for hop in range(1, hops + 1):
            for d, half in lanes(hop):
                gather_passed(st, d, hop, half).wait()
                gather_send(st, d, hop, half).wait_send()

    def forward(st):
        for i in range(NFWD):
            fwd[st, i] = everyone[st, tab[FWD + i]]
            copy(fwd.at[st, i], got.at[st, i], fs.at[i], fr.at[i], after).start()

    def forwarded(st):
        for i in range(NFWD):
            copy(fwd.at[st, i], got.at[st, i], fs.at[i], fr.at[i], after).wait()

    state[...] = f_ref[...]
    for d, dist in paths:
        if dist <= reach:
            for side in range(2):
                coord_got(d, dist, side).wait_recv()
            if dist == reach and hops > reach:
                for far in range(hops, reach, -1):
                    if (d, far) in paths:
                        for side in range(2):
                            coord_send(d, far, side).start()
    for d, dist in paths:
        if dist > reach:
            for side in range(2):
                coord_got(d, dist, side).wait_recv()
    other = cx.at[me + 1 - 2 * core]
    copy(other, other, cps.at[0], cpr.at[0], partner).wait()
    for d, dist in paths:
        for side in range(2):
            coord_send(d, dist, side).wait_send()
    for i in range(NFWD):
        fxs[i] = cx[tab[FWD + i] // 2]
        copy(fxs.at[i], fx.at[i], xfs.at[i], xfr.at[i], after).start()
    gather_begin(0)

    lane8 = lax.broadcasted_iota(jnp.int32, (8, 2 * B), 1)
    sub8 = lax.broadcasted_iota(jnp.int32, (8, 2 * B), 0)
    lane = lax.broadcasted_iota(jnp.int32, (B, 2 * B), 1)
    sub = lax.broadcasted_iota(jnp.int32, (B, 2 * B), 0)
    point = jnp.where(lane < B, lane, lane - B)

    def mask(half, slot):
        return tab[MASK + half * NCOND + slot].astype(F32)

    def stand(j):
        if j == NCOND:
            placed = jnp.where(sub8 == 3, 1.0, x_ref[...])
        else:
            sides = []
            for half in range(2):
                if j < NSAME:
                    row = tab[half * NSAME + j]
                    found, side = cx[row // 2], row % 2
                else:
                    i = half * NCROSS + j - NSAME
                    found, side = fx[i], tab[HALF + i]
                turned = jnp.concatenate([found[:, B:], found[:, :B]], axis=1)
                same = (side == half).astype(F32)
                sides.append(found * same + turned * (1.0 - same))
            placed = jnp.where(lane8 < B, sides[0], sides[1])
            weights = jnp.where(lane8 < B, mask(0, j), mask(1, j))
            placed = jnp.where(sub8 == 3, weights, placed)
        xcol[j] = placed
        standing = placed.T
        for d in range(4):
            xrow[d, j * B : (j + 1) * B] = jnp.where(
                lane < B, standing[:B, d : d + 1], standing[B:, d : d + 1]
            )
    def fill(j, low, high):
        sq = None
        for d in range(3):
            diff = xrow[d, low * B : high * B] - xcol[j, d : d + 1]
            sq = diff * diff if sq is None else sq + diff * diff
        weights = xcol[j, 3:4]
        s_ref[j, low * B : high * B] = (
            jnp.exp(-jnp.sqrt(sq) / LENGTH_SCALE) * xrow[3, low * B : high * B] * weights
        )
        if low == j:
            s_ref[j, j * B : (j + 1) * B] += jnp.where(
                sub == point, NUGGET * weights + (1.0 - weights), 0.0
            )

    early = list(range(NSAME)) + [NCOND]
    for j in early:
        stand(j)
    for j in early:
        if j < NSAME:
            fill(j, j, NSAME)
        fill(j, NCOND, NB)
    for i in range(NFWD):
        copy(fxs.at[i], fx.at[i], xfs.at[i], xfr.at[i], after).wait()
    for j in range(NSAME, NCOND):
        stand(j)
    for j in range(NCOND):
        if j < NSAME:
            fill(j, NSAME, NCOND)
        else:
            fill(j, j, NB)

    def eliminate(j, carry):
        inv = invert_pair(s_ref[j, pl.ds(pl.multiple_of(j * B, B), B)])
        prec_ref[...] = inv
        big = diag_pair(inv)
        for jj in range(NCOND):

            @pl.when(j == jj)
            def _():
                if 1 <= jj <= hops // 2:
                    gather_next(0, 2 * jj)
                panel = s_ref[jj, (jj + 1) * B :]
                w = dot(panel, big, NN)
                for i in range(jj + 1, NB):
                    o = (i - jj - 1) * B
                    s_ref[i, i * B :] -= dot(w[o:], diag_pair(panel[o : o + B]), NT)
                s_ref[jj, (jj + 1) * B :] = w

        return carry

    lax.fori_loop(0, NB, eliminate, 0)
    gather_end(0)
    forward(0)
    own = NCOND * B
    rest = [s_ref[j, own:] for j in range(NCOND)]
    for i in range(NCOND - 1, -1, -1):
        kept = rest[i] * jnp.where(lane < B, mask(0, i), mask(1, i))
        turned = kept.T
        for half in range(2):
            high, low = split(kept[:, half * B : (half + 1) * B])
            reg_ref[half, :B, i * B : (i + 1) * B] = high
            reg_ref[half, B:, i * B : (i + 1) * B] = low
            high, low = split(turned[half * B : (half + 1) * B])
            for part, values in enumerate((high, low, high)):
                regt_ref[half, i * B : (i + 1) * B, part * B : (part + 1) * B] = values
        for j in range(i):
            rest[j] = rest[j] - dot(rest[i], diag_pair(s_ref[j, i * B : (i + 1) * B]), NN)

    for st in range(STEPS):
        if st:
            gather_begin(st)
            for hop in range(2, hops + 1, 2):
                gather_next(st, hop)
            gather_end(st)
            forward(st)
        width = NSAME * B

        def seen(cond, first, last):
            both = plain(reg_ref[half, :, first:last], jnp.concatenate(cond, axis=0))
            return both[:B] + both[B:]

        def stacked(values):
            high, low = split(values)
            return jnp.concatenate([high, high, low], axis=0)

        for half in range(2):
            cond = [everyone[st, tab[half * NSAME + s]] for s in range(NSAME)]
            scaled[half] = state[half] - seen(cond, 0, width)
        forwarded(st)
        parts = []
        for half in range(2):
            cond = [got[st, half * NCROSS + s] for s in range(NCROSS)]
            resid = scaled[half] - seen(cond, width, NCOND * B)
            solved = dot(prec_ref[:, half * B : (half + 1) * B], resid, NN)
            scaled[half] = solved
            parts.append(stacked(solved))
            terms = plain(regt_ref[half, width:], parts[half])
            for s in range(NCROSS):
                i = half * NCROSS + s
                home[st, i] = terms[s * B : (s + 1) * B].astype(BF16)
                copy(home.at[st, i], back.at[st, FWD + i], bs.at[i], br.at[i], before).start()
        for half in range(2):
            terms = plain(regt_ref[half, :width], parts[half])
            for s in range(NSAME):
                back[st, half * NSAME + s] = terms[s * B : (s + 1) * B].astype(BF16)
        back[st, SLOTS] = jnp.zeros((B, back.shape[3]), BF16)
        for i in range(NFWD):
            copy(home.at[st, i], back.at[st, FWD + i], bs.at[i], br.at[i], before).wait()

        order = [around(hops)]
        for step in range(hops - 1, 0, -1):
            order += [around(step), around(-step)]
        order.append(chip)

        def given(n):
            ref = give_buf.at[st, n]
            return copy(ref, take_buf.at[st, n], vs.at[n], vr.at[n], partner)

        for n, dest in enumerate(order):
            give_buf[st, n] = back[st, tab[give + dest]]
            given(n).start()

        def owed(n, half):
            dest = order[n]
            mine = back[st, tab[SEL + 4 * dest + 2 * core + half]].astype(F32)
            return mine + take_buf[st, n].astype(F32) * tab[take + 2 * dest + half].astype(F32)

        def carried(d, hop, half):
            return copy(
                out_buf.at[st, d, hop - 1, half], in_buf.at[st, d, hop - 1, half],
                rs.at[d, hop - 1, half], rr.at[d, hop - 1, half],
                along(sign[d] * (2 - hop % 2), core),
            )

        def starts(hop):
            return [(d, half) for half in range(2) for d in range(2) if hop < hops or d == half]

        def arrived(d, hop, half):
            carried(d, hop, half).wait_recv()
            return in_buf[st, d, hop - 1, half].astype(F32)

        def place(d, hop):
            return 0 if hop == hops else 2 * (hops - hop) - 1 + d

        for hop in range(hops, 0, -1):
            for n in sorted({place(d, hop) for d in range(2)}):
                given(n).wait_recv()
            for d, half in starts(hop):
                total = owed(place(d, hop), half)
                if hop % 2 == 0 and hop < hops:
                    total = total + arrived(d, hop + 1, half)
                    if (d, half) in starts(hop + 2):
                        total = total + arrived(d, hop + 2, half)
                out_buf[st, d, hop - 1, half] = total.astype(BF16)
                carried(d, hop, half).start()
        last = 2 * hops - 1
        given(last).wait_recv()
        for half in range(2):
            incoming = owed(last, half)
            for d in range(2):
                for hop in (1, 2):
                    if (d, half) in starts(hop):
                        incoming = incoming + arrived(d, hop, half)
            now = state[half]
            grad = jnp.tanh(y_ref[half] - now) - (scaled[half] - incoming)
            state[half] = now + STEP_SIZE * grad
            grad_ref[half] = grad
        for n in range(2 * hops):
            given(n).wait_send()
        for hop in range(1, hops + 1):
            for d, half in starts(hop):
                carried(d, hop, half).wait_send()
    field_ref[...] = state[...]


def body(coords, field, observed, pair_owner, cond_list, cond_mask):
    groups = lax.axis_size("grp")
    members = lax.axis_size("dev")
    chips = members // 2
    hops = chips // 2
    group = lax.axis_index("grp")
    following = jnp.minimum(group + 1, groups - 1)
    has_next = (group + 1 < groups).astype(jnp.int32)
    cols = field.shape[1]
    lists = cond_list.reshape(groups, 2 * members, NCOND).transpose(0, 2, 1)
    masks = cond_mask.reshape(groups, 2 * members, NCOND).transpose(0, 2, 1)

    def both(array):
        return jnp.stack([array[group], array[following]])

    masks = both(masks) * jnp.stack([jnp.int32(1), has_next])[:, None, None]
    size = offsets(chips)[2]
    smem = pl.BlockSpec(memory_space=pltpu.SMEM)
    vmem = pl.BlockSpec(memory_space=pltpu.VMEM)
    x = jnp.pad(coords, ((0, 5), (0, 0)))
    sem = pltpu.SemaphoreType.DMA
    block = (B, cols)
    shape = (2, B, cols)
    out = pl.pallas_call(
        main_kernel,
        out_shape=(jax.ShapeDtypeStruct(shape, F32), jax.ShapeDtypeStruct(shape, F32)),
        in_specs=[smem, smem, smem, vmem, vmem, vmem],
        out_specs=(vmem, vmem),
        scratch_shapes=[
            pltpu.SMEM((size,), jnp.int32),
            pltpu.SMEM((2 * SLOTS,), jnp.int32),
            pltpu.VMEM((members, 8, 2 * B), F32),
            pltpu.VMEM((NFWD, 8, 2 * B), F32),
            pltpu.VMEM((NFWD, 8, 2 * B), F32),
            pltpu.VMEM((NB, 8, 2 * B), F32),
            pltpu.VMEM((4, NB * B, 2 * B), F32),
            pltpu.VMEM((NB, NB * B, 2 * B), F32),
            pltpu.VMEM((B, 2 * B), F32),
            pltpu.VMEM((2, 2 * B, NCOND * B), BF16),
            pltpu.VMEM((2, NCOND * B, 3 * B), BF16),
            pltpu.VMEM(shape, F32),
            pltpu.VMEM(shape, F32),
            pltpu.VMEM((STEPS, 2 * members) + block, BF16),
            pltpu.VMEM((STEPS, NFWD) + block, BF16),
            pltpu.VMEM((STEPS, NFWD) + block, BF16),
            pltpu.VMEM((STEPS, SLOTS + 1) + block, BF16),
            pltpu.VMEM((STEPS, NFWD) + block, BF16),
            pltpu.VMEM((STEPS, chips) + block, BF16),
            pltpu.VMEM((STEPS, chips) + block, BF16),
            pltpu.VMEM((STEPS, 2, hops, 2) + block, BF16),
            pltpu.VMEM((STEPS, 2, hops, 2) + block, BF16),
            sem((2, hops, 2)), sem((2, hops, 2)),
            sem((1,)), sem((1,)),
            sem((NFWD,)), sem((NFWD,)),
            sem((2, hops, 2)), sem((2, hops, 2)),
            sem((2, hops + 1, 2)), sem((2, hops + 1, 2)),
            sem((NFWD,)), sem((NFWD,)),
            sem((NFWD,)), sem((NFWD,)),
            sem((chips,)), sem((chips,)),
            sem((2, hops, 2)), sem((2, hops, 2)),
        ],
        compiler_params=pltpu.CompilerParams(
            collective_id=0, has_side_effects=True, vmem_limit_bytes=48 * 1024 * 1024
        ),
        name="vecchia",
    )(both(pair_owner), both(lists), masks, x, field.reshape(shape), observed.reshape(shape))
    return tuple(array.reshape(2 * B, cols) for array in out)


def solution(mesh):
    placed = (
        P(None, ("grp", "dev")),
        P(("grp", "dev"), None),
        P(("grp", "dev"), None),
        P(),
        P(),
        P(),
    )
    return jax.shard_map(
        body,
        mesh=mesh,
        in_specs=placed,
        out_specs=(P(("grp", "dev"), None), P(("grp", "dev"), None)),
        check_vma=False,
    )
```

time: 203 us -> 160 us (0.79)
  the two profiles are of different devices: /device:TPU:62 before, /device:TPU:30 now
where the time goes in v3:
time: 160 us
  Pallas kernels  156 us (98%)
  local copies, waits for them, and re-layouts  3.65 us (2%)
    pallas_call x1, Pallas kernels, body(): pl.pallas_call(main_kernel, out_shape=(jax.ShapeDtypeStruct(shape, F32),...  156 us

profile of v3, /device:TPU:30, one launch (start us, length us, event | category | flops | bytes accessed | tf_op | source)
XLA Modules:
  0.0 160.1 jit_solution(1322872965134379693)
XLA Ops:
  0.6 0.0 copy-start.2
  0.6 0.1 add_convert_fusion
  0.7 0.0 copy-start.3
  0.7 0.8 constant_dynamic-slice_fusion.5
  1.5 0.7 pad.4.x_ref
  2.2 0.0 copy-done.2
  2.2 0.0 copy-start
  2.2 0.0 copy-start.1
  2.2 0.1 reshape.23
  2.3 0.0 copy-done.3
  2.3 0.1 reshape.24
  2.4 0.1 add_multiply_fusion.mask_ref
  2.5 0.6 copy-done
  3.1 0.1 copy-done.1
  3.2 155.6 %vecchia.1 = (f32[2,64,256]{2,1,0:T(8,128)S(1)}, f32[2,64,256]{2,1,0:T(8,128)S(1)}) custom-call(s32[2,32]{1,0:T(2,128)S(1)} %pad_add_fusion.1.owner_ref, s32[2,8,64]{2,1,0:T(8,128)S(1)} %pad_add_fusion.list_ref, s32[2,8,64]{2,1,0:T(8,128)S(1)} %add_multiply_fusion.mask_ref, f32[8,128]{1,0:T(8,128)S(1)} %pad.4.x_ref, f32[2,64,256]{2,1,0:T(8,128)S(1)} %bitcast.21, ...), custom_call_target="tpu_custom_call" | custom-call | tf_op jit(solution)/shard_map/vecchia/pallas_call | solution.py:542
  158.8 0.7 copy.18
  159.4 0.7 copy.19
  (3 shorter events, 0.0 us)
Async XLA Ops:
  0.6 1.6 copy-start.2
  0.7 1.6 copy-start.3
  2.2 0.9 copy-start
  2.2 1.0 copy-start.1
